TPU v7x, 32 devices: a whole 2x2x4 slice. The times are simulated.
32 devices in a mesh: ctx: 16 (over z, y, core), fsdp: 2 (over x).
Axes of the slice: x: 2, y: 2, z: 4, core: 2. Of those that a mesh axis runs over, the one named last changes fastest.
Arguments:
- tokens: bfloat16 [8192, 768], P(('ctx', 'fsdp')), may hold values from -6 to 6
- cotangent: bfloat16 [8192, 768], P(('ctx', 'fsdp')), may hold values from -6 to 6
- doc_lengths: int32 [4], replicated, may hold values from 1 to 4096, 8192 in all
- deal: int32 [64], replicated, may hold values from 0 to 63, each once
- first_gain: bfloat16 [768], P('fsdp'), may hold values from 0.5 to 1.5
- first_shift: bfloat16 [768], P('fsdp'), may hold values from -4 to 4
- query_weight: bfloat16 [768, 768], P('fsdp'), may hold values from -0.21875 to 0.21875
- query_bias: bfloat16 [768], P('fsdp'), may hold values from -6 to 6
- key_weight: bfloat16 [768, 768], P('fsdp'), may hold values from -0.21875 to 0.21875
- value_weight: bfloat16 [768, 768], P('fsdp'), may hold values from -0.21875 to 0.21875
- value_bias: bfloat16 [768], P('fsdp'), may hold values from -0.75 to 0.75
- output_weight: bfloat16 [768, 768], P('fsdp'), may hold values from -3.5 to 3.5
- output_bias: bfloat16 [768], P('fsdp'), may hold values from -4 to 4
- second_gain: bfloat16 [768], P('fsdp'), may hold values from 0.5 to 1.5
- second_shift: bfloat16 [768], P('fsdp'), may hold values from -4 to 4
- up_weight: bfloat16 [768, 3072], P('fsdp'), may hold values from -0.21875 to 0.21875
- up_bias: bfloat16 [3072], P('fsdp'), may hold values from -4 to 4
- down_weight: bfloat16 [3072, 768], P('fsdp'), may hold values from -0.109375 to 0.109375
- down_bias: bfloat16 [768], P('fsdp'), may hold values from -4 to 4
Outputs:
- result: bfloat16 [8192, 768], P(('ctx', 'fsdp'))
- grad_tokens: float32 [8192, 768], P(('ctx', 'fsdp'))
- grad_first_gain: float32 [768], P('fsdp')
- grad_first_shift: float32 [768], P('fsdp')
- grad_query_weight: float32 [768, 768], P('fsdp')
- grad_query_bias: float32 [768], P('fsdp')
- grad_key_weight: float32 [768, 768], P('fsdp')
- grad_value_weight: float32 [768, 768], P('fsdp')
- grad_value_bias: float32 [768], P('fsdp')
- grad_output_weight: float32 [768, 768], P('fsdp')
- grad_output_bias: float32 [768], P('fsdp')
- grad_second_gain: float32 [768], P('fsdp')
- grad_second_shift: float32 [768], P('fsdp')
- grad_up_weight: float32 [768, 3072], P('fsdp')
- grad_up_bias: float32 [3072], P('fsdp')
- grad_down_weight: float32 [3072, 768], P('fsdp')
- grad_down_bias: float32 [768], P('fsdp')
Inputs may be any that keep to these rules, and one draw needn't show every extreme that they name: Slot j of the 64 slots holds text block deal[j]; every block stands in exactly one slot. `doc_lengths`: the documents in text order; their lengths sum to 8192.
All inputs are finite; a program needn't handle non-finite values.
Results may differ from a plain program's by a relative error of at most 0.014.
Values may be sent and summed in bfloat16 or wider, within the bound.
A program may use at most 384 MiB of HBM per device.

v0:
```python
import jax
import jax.numpy as jnp
from jax import lax
from jax.sharding import PartitionSpec as P

HEADS = 12
DH = 64
NSUM = 50
SEG = 2048
DOC_MAX = 4096


EPS = 1e-05
SCALE = 0.125
MASKED = -1e30
ROOT_HALF = 0.7071067811865476


def smooth_unit(values):
    return 0.5 * values * (1.0 + jax.scipy.special.erf(values * ROOT_HALF))


def layer_norm(values, gain, shift):
    mean = jnp.mean(values, axis=-1, keepdims=True)
    centred = values - mean
    spread = jnp.mean(centred * centred, axis=-1, keepdims=True)
    return centred * lax.rsqrt(spread + EPS) * gain + shift


def describe(positions, doc_lengths):
    starts = jnp.cumsum(doc_lengths) - doc_lengths
    before = starts <= positions[..., None]
    begin = jnp.max(jnp.where(before, starts, jnp.int32(0)), axis=-1)
    within = positions - begin
    period = jnp.int32(SEG + NSUM)
    return (positions, begin, within // period, within % period >= SEG)


def permitted(query, key):
    same_doc = query[1][:, None] == key[1][None, :]
    causal = (key[0][None, :] <= query[0][:, None]) & (key[0][None, :] >= 0)
    visible = (key[2][None, :] == query[2][:, None]) | key[3][None, :]
    return same_doc & causal & visible


def outer(left, right):
    return lax.dot_general(
        left, right, (((0,), (0,)), ((), ())), preferred_element_type=jnp.float32
    )


def inner(left, right):
    return lax.dot_general(
        left, right, (((1,), (1,)), ((), ())), preferred_element_type=jnp.float32
    )


def head_slice(values, head):
    return lax.dynamic_slice_in_dim(values, head * DH, DH, 1)


def merge_heads(values):
    return values.transpose(1, 0, 2).reshape(values.shape[1], -1)


def make_collect(deal, mine, block, reach, offset, along, carry, piece):
    blocks_here = piece[0].shape[along] // block

    def take(number, held):
        held = list(held)
        label = lax.dynamic_index_in_dim(deal, number, keepdims=False)
        for index in range(2):
            place = label - mine[index] + offset
            inside = (place >= 0) & (place <= reach)
            spot = jnp.clip(place, 0, reach)
            for member in range(len(held)):
                fresh = lax.dynamic_slice_in_dim(piece[member], number * block, block, along)
                current = held[member][index, spot]
                held[member] = held[member].at[index, spot].set(jnp.where(inside, fresh, current))
        return tuple(held)

    return lax.fori_loop(0, blocks_here, take, carry)


def attend_forward(queries, keys, values, permit):

    def attend_one_head(head):
        scores = jnp.where(permit, inner(head_slice(queries, head), head_slice(keys, head)), MASKED)
        top = jnp.max(scores, axis=1, keepdims=True)
        expo = jnp.exp(scores - top)
        total = jnp.sum(expo, axis=1, keepdims=True)
        probs = (expo / total).astype(jnp.bfloat16)
        return (
            jnp.dot(probs, head_slice(values, head), preferred_element_type=jnp.float32),
            top[:, 0],
            total[:, 0],
        )

    outputs, tops, totals = lax.map(attend_one_head, jnp.arange(HEADS, dtype=jnp.int32))
    return (merge_heads(outputs), tops, totals)


def query_backward(queries, keys, values, permit, grad_out, tops, totals):

    def query_one_head(head):
        query_head = head_slice(queries, head)
        key_head = head_slice(keys, head)
        value_head = head_slice(values, head)
        grad_head = head_slice(grad_out, head)
        scores = jnp.where(permit, inner(query_head, key_head), MASKED)
        top = lax.dynamic_index_in_dim(tops, head, keepdims=False)[:, None]
        total = lax.dynamic_index_in_dim(totals, head, keepdims=False)[:, None]
        probs = jnp.exp(scores - top) / total
        dprob = inner(grad_head, value_head)
        delta = jnp.sum(probs * dprob, axis=1, keepdims=True)
        dscore = (probs * (dprob - delta)).astype(jnp.bfloat16)
        grad_query = jnp.dot(dscore, key_head, preferred_element_type=jnp.float32)
        return (grad_query, delta[:, 0])

    grad_query, deltas = lax.map(query_one_head, jnp.arange(HEADS, dtype=jnp.int32))
    return (merge_heads(grad_query), deltas)


def key_backward(
    held_queries, held_grads, held_tops, held_totals, held_deltas, keys, values, permit
):
    span = held_queries.shape[0]

    def key_one_head(head):
        query_head = head_slice(held_queries, head)
        grad_head = head_slice(held_grads, head)
        key_head = head_slice(keys, head)
        value_head = head_slice(values, head)
        scores = jnp.where(permit, inner(query_head, key_head), MASKED)
        top = lax.dynamic_index_in_dim(held_tops, head, 1, keepdims=False).reshape(span, 1)
        total = lax.dynamic_index_in_dim(held_totals, head, 1, keepdims=False).reshape(span, 1)
        delta = lax.dynamic_index_in_dim(held_deltas, head, 1, keepdims=False).reshape(span, 1)
        probs = jnp.exp(scores - top) / total
        dprob = inner(grad_head, value_head)
        dscore = (probs * (dprob - delta)).astype(jnp.bfloat16)
        grad_key = outer(dscore, query_head)
        grad_value = outer(probs.astype(jnp.bfloat16), grad_head)
        return (grad_key, grad_value)

    grad_key, grad_value = lax.map(key_one_head, jnp.arange(HEADS, dtype=jnp.int32))
    return (merge_heads(grad_key), merge_heads(grad_value))


def shards(
    tokens,
    cotangent,
    doc_lengths,
    deal,
    first_gain,
    first_shift,
    query_weight,
    query_bias,
    key_weight,
    value_weight,
    value_bias,
    output_weight,
    output_bias,
    second_gain,
    second_shift,
    up_weight,
    up_bias,
    down_weight,
    down_bias,
):
    whole = (
        lax.all_gather(first_gain, "fsdp", axis=0, tiled=True),
        lax.all_gather(first_shift, "fsdp", axis=0, tiled=True),
        lax.all_gather(query_weight, "fsdp", axis=0, tiled=True),
        lax.all_gather(query_bias, "fsdp", axis=0, tiled=True),
        lax.all_gather(key_weight, "fsdp", axis=0, tiled=True),
        lax.all_gather(value_weight, "fsdp", axis=0, tiled=True),
        lax.all_gather(value_bias, "fsdp", axis=0, tiled=True),
        lax.all_gather(output_weight, "fsdp", axis=0, tiled=True),
        lax.all_gather(output_bias, "fsdp", axis=0, tiled=True),
        lax.all_gather(second_gain, "fsdp", axis=0, tiled=True),
        lax.all_gather(second_shift, "fsdp", axis=0, tiled=True),
        lax.all_gather(up_weight, "fsdp", axis=0, tiled=True),
        lax.all_gather(up_bias, "fsdp", axis=0, tiled=True),
        lax.all_gather(down_weight, "fsdp", axis=0, tiled=True),
        lax.all_gather(down_bias, "fsdp", axis=0, tiled=True),
    )
    (
        lower_gain,
        lower_shift,
        query_mat,
        query_add,
        key_mat,
        value_mat,
        value_add,
        output_mat,
        output_add,
        upper_gain,
        upper_shift,
        expand_mat,
        expand_add,
        reduce_mat,
        reduce_add,
    ) = whole
    lower_gain = lower_gain.astype(jnp.float32)
    lower_shift = lower_shift.astype(jnp.float32)
    query_add = query_add.astype(jnp.float32)
    value_add = value_add.astype(jnp.float32)
    output_add = output_add.astype(jnp.float32)
    upper_gain = upper_gain.astype(jnp.float32)
    upper_shift = upper_shift.astype(jnp.float32)
    expand_add = expand_add.astype(jnp.float32)
    reduce_add = reduce_add.astype(jnp.float32)
    rows = tokens.shape[0]
    width = tokens.shape[1]
    block = rows // 2
    reach = DOC_MAX // block
    span = (reach + 1) * block
    count_slots = deal.shape[0]
    here = lax.axis_index(("ctx", "fsdp"))
    mine = lax.dynamic_slice_in_dim(deal, here * 2, 2)
    offsets = jnp.arange(block, dtype=jnp.int32)
    steps_back = jnp.arange(reach + 1, dtype=jnp.int32)
    key_blocks = mine[:, None] - reach + steps_back[None, :]
    query_blocks = mine[:, None] + steps_back[None, :]
    permits = []
    back_permits = []
    for index in range(2):
        own_info = describe(mine[index] * block + offsets, doc_lengths)
        key_info = describe(
            (key_blocks[index][:, None] * block + offsets[None, :]).reshape(-1), doc_lengths
        )
        permits.append(permitted(own_info, key_info))
        later_info = describe(
            (query_blocks[index][:, None] * block + offsets[None, :]).reshape(-1), doc_lengths
        )
        later_valid = jnp.repeat(query_blocks[index] < count_slots, block)
        back_permits.append(permitted(later_info, own_info) & later_valid[:, None])
    inputs = tokens.astype(jnp.float32)
    first_normed = layer_norm(inputs, lower_gain, lower_shift).astype(jnp.bfloat16)
    queries = (
        (jnp.dot(first_normed, query_mat, preferred_element_type=jnp.float32) + query_add) * SCALE
    ).astype(jnp.bfloat16)
    keys = jnp.dot(first_normed, key_mat, preferred_element_type=jnp.float32).astype(jnp.bfloat16)
    values = (
        jnp.dot(first_normed, value_mat, preferred_element_type=jnp.float32) + value_add
    ).astype(jnp.bfloat16)
    empty = jnp.zeros((2, reach + 1, block, width), jnp.bfloat16)
    held_keys, held_values = make_collect(
        deal,
        mine,
        block,
        reach,
        reach,
        0,
        (empty, empty),
        (
            lax.all_gather(keys, ("ctx", "fsdp"), axis=0, tiled=True),
            lax.all_gather(values, ("ctx", "fsdp"), axis=0, tiled=True),
        ),
    )
    mixed_parts = []
    top_parts = []
    total_parts = []
    for index in range(2):
        local_q = queries[index * block : (index + 1) * block]
        mixed, tops, totals = attend_forward(
            local_q,
            held_keys[index].reshape(span, width),
            held_values[index].reshape(span, width),
            permits[index],
        )
        mixed_parts.append(mixed)
        top_parts.append(tops)
        total_parts.append(totals)
    attn = jnp.concatenate(mixed_parts, axis=0).astype(jnp.bfloat16)
    middle = inputs + jnp.dot(attn, output_mat, preferred_element_type=jnp.float32) + output_add
    second_normed = layer_norm(middle, upper_gain, upper_shift).astype(jnp.bfloat16)
    expanded = jnp.dot(second_normed, expand_mat, preferred_element_type=jnp.float32) + expand_add
    hidden = smooth_unit(expanded).astype(jnp.bfloat16)
    result = (
        middle + jnp.dot(hidden, reduce_mat, preferred_element_type=jnp.float32) + reduce_add
    ).astype(jnp.bfloat16)
    grad_in = cotangent.astype(jnp.float32)
    term_reduce_mat = outer(hidden, cotangent)
    term_reduce_add = jnp.sum(grad_in, axis=0)
    grad_hidden = inner(cotangent, reduce_mat).astype(jnp.bfloat16)
    unused_unit, pull_unit = jax.vjp(smooth_unit, expanded)
    grad_expand = pull_unit(grad_hidden.astype(jnp.float32))[0].astype(jnp.bfloat16)
    term_expand_mat = outer(second_normed, grad_expand)
    term_expand_add = jnp.sum(grad_expand.astype(jnp.float32), axis=0)
    grad_second = inner(grad_expand, expand_mat)
    unused, pull_second = jax.vjp(layer_norm, middle, upper_gain, upper_shift)
    grad_middle_part, term_upper_gain, term_upper_shift = pull_second(grad_second)
    grad_middle = grad_in + grad_middle_part
    grad_branch = grad_middle.astype(jnp.bfloat16)
    term_output_mat = outer(attn, grad_branch)
    term_output_add = jnp.sum(grad_branch.astype(jnp.float32), axis=0)
    grad_mixed = inner(grad_branch, output_mat).astype(jnp.bfloat16)
    query_parts = []
    delta_parts = []
    for index in range(2):
        local_q = queries[index * block : (index + 1) * block]
        local_grad = grad_mixed[index * block : (index + 1) * block]
        grad_query, deltas = query_backward(
            local_q,
            held_keys[index].reshape(span, width),
            held_values[index].reshape(span, width),
            permits[index],
            local_grad,
            top_parts[index],
            total_parts[index],
        )
        query_parts.append(grad_query)
        delta_parts.append(deltas)
    grad_query = jnp.concatenate(query_parts, axis=0)
    all_tops = jnp.concatenate(top_parts, axis=1)
    all_totals = jnp.concatenate(total_parts, axis=1)
    all_deltas = jnp.concatenate(delta_parts, axis=1)
    empty_rows = jnp.zeros((2, reach + 1, block, width), jnp.bfloat16)
    held_queries, held_grads = make_collect(
        deal,
        mine,
        block,
        reach,
        0,
        0,
        (empty_rows, empty_rows),
        (
            lax.all_gather(queries, ("ctx", "fsdp"), axis=0, tiled=True),
            lax.all_gather(grad_mixed, ("ctx", "fsdp"), axis=0, tiled=True),
        ),
    )
    zero_stats = jnp.zeros((2, reach + 1, HEADS, block), jnp.float32)
    one_stats = jnp.ones((2, reach + 1, HEADS, block), jnp.float32)
    held_tops, held_totals, held_deltas = make_collect(
        deal,
        mine,
        block,
        reach,
        0,
        1,
        (zero_stats, one_stats, zero_stats),
        (
            lax.all_gather(all_tops, ("ctx", "fsdp"), axis=1, tiled=True),
            lax.all_gather(all_totals, ("ctx", "fsdp"), axis=1, tiled=True),
            lax.all_gather(all_deltas, ("ctx", "fsdp"), axis=1, tiled=True),
        ),
    )
    key_grad_parts = []
    value_grad_parts = []
    for index in range(2):
        own_keys = keys[index * block : (index + 1) * block]
        own_values = values[index * block : (index + 1) * block]
        grad_key, grad_value = key_backward(
            held_queries[index].reshape(span, width),
            held_grads[index].reshape(span, width),
            held_tops[index],
            held_totals[index],
            held_deltas[index],
            own_keys,
            own_values,
            back_permits[index],
        )
        key_grad_parts.append(grad_key)
        value_grad_parts.append(grad_value)
    grad_keys = jnp.concatenate(key_grad_parts, axis=0).astype(jnp.bfloat16)
    grad_values = jnp.concatenate(value_grad_parts, axis=0).astype(jnp.bfloat16)
    grad_scaled = grad_query.astype(jnp.bfloat16) * jnp.bfloat16(SCALE)
    term_query_mat = outer(first_normed, grad_scaled)
    term_query_add = jnp.sum(grad_scaled.astype(jnp.float32), axis=0)
    term_key_mat = outer(first_normed, grad_keys)
    term_value_mat = outer(first_normed, grad_values)
    term_value_add = jnp.sum(grad_values.astype(jnp.float32), axis=0)
    grad_first = (
        inner(grad_scaled, query_mat) + inner(grad_keys, key_mat) + inner(grad_values, value_mat)
    )
    unused_first, pull_first = jax.vjp(layer_norm, inputs, lower_gain, lower_shift)
    grad_input_part, term_lower_gain, term_lower_shift = pull_first(grad_first)
    grad_tokens = grad_middle + grad_input_part
    terms = (
        term_lower_gain,
        term_lower_shift,
        term_query_mat,
        term_query_add,
        term_key_mat,
        term_value_mat,
        term_value_add,
        term_output_mat,
        term_output_add,
        term_upper_gain,
        term_upper_shift,
        term_expand_mat,
        term_expand_add,
        term_reduce_mat,
        term_reduce_add,
    )
    summed = lax.psum(
        (
            terms[0],
            terms[1],
            terms[2],
            terms[3],
            terms[4],
            terms[5],
            terms[6],
            terms[7],
            terms[8],
            terms[9],
            terms[10],
            terms[11],
            terms[12],
            terms[13],
            terms[14],
        ),
        "ctx",
    )
    owned = (
        lax.psum_scatter(
            summed[0].astype(jnp.bfloat16), "fsdp", scatter_dimension=0, tiled=True
        ).astype(jnp.float32),
        lax.psum_scatter(
            summed[1].astype(jnp.bfloat16), "fsdp", scatter_dimension=0, tiled=True
        ).astype(jnp.float32),
        lax.psum_scatter(
            summed[2].astype(jnp.bfloat16), "fsdp", scatter_dimension=0, tiled=True
        ).astype(jnp.float32),
        lax.psum_scatter(
            summed[3].astype(jnp.bfloat16), "fsdp", scatter_dimension=0, tiled=True
        ).astype(jnp.float32),
        lax.psum_scatter(
            summed[4].astype(jnp.bfloat16), "fsdp", scatter_dimension=0, tiled=True
        ).astype(jnp.float32),
        lax.psum_scatter(
            summed[5].astype(jnp.bfloat16), "fsdp", scatter_dimension=0, tiled=True
        ).astype(jnp.float32),
        lax.psum_scatter(
            summed[6].astype(jnp.bfloat16), "fsdp", scatter_dimension=0, tiled=True
        ).astype(jnp.float32),
        lax.psum_scatter(
            summed[7].astype(jnp.bfloat16), "fsdp", scatter_dimension=0, tiled=True
        ).astype(jnp.float32),
        lax.psum_scatter(
            summed[8].astype(jnp.bfloat16), "fsdp", scatter_dimension=0, tiled=True
        ).astype(jnp.float32),
        lax.psum_scatter(
            summed[9].astype(jnp.bfloat16), "fsdp", scatter_dimension=0, tiled=True
        ).astype(jnp.float32),
        lax.psum_scatter(
            summed[10].astype(jnp.bfloat16), "fsdp", scatter_dimension=0, tiled=True
        ).astype(jnp.float32),
        lax.psum_scatter(
            summed[11].astype(jnp.bfloat16), "fsdp", scatter_dimension=0, tiled=True
        ).astype(jnp.float32),
        lax.psum_scatter(
            summed[12].astype(jnp.bfloat16), "fsdp", scatter_dimension=0, tiled=True
        ).astype(jnp.float32),
        lax.psum_scatter(
            summed[13].astype(jnp.bfloat16), "fsdp", scatter_dimension=0, tiled=True
        ).astype(jnp.float32),
        lax.psum_scatter(
            summed[14].astype(jnp.bfloat16), "fsdp", scatter_dimension=0, tiled=True
        ).astype(jnp.float32),
    )
    return (
        result,
        grad_tokens,
        owned[0],
        owned[1],
        owned[2],
        owned[3],
        owned[4],
        owned[5],
        owned[6],
        owned[7],
        owned[8],
        owned[9],
        owned[10],
        owned[11],
        owned[12],
        owned[13],
        owned[14],
    )


def solution(mesh):
    in_specs = (
        P(("ctx", "fsdp"), None),
        P(("ctx", "fsdp"), None),
        P(),
        P(),
        P("fsdp"),
        P("fsdp"),
        P("fsdp", None),
        P("fsdp"),
        P("fsdp", None),
        P("fsdp", None),
        P("fsdp"),
        P("fsdp", None),
        P("fsdp"),
        P("fsdp"),
        P("fsdp"),
        P("fsdp", None),
        P("fsdp"),
        P("fsdp", None),
        P("fsdp"),
    )
    out_specs = (
        P(("ctx", "fsdp"), None),
        P(("ctx", "fsdp"), None),
        P("fsdp"),
        P("fsdp"),
        P("fsdp", None),
        P("fsdp"),
        P("fsdp", None),
        P("fsdp", None),
        P("fsdp"),
        P("fsdp", None),
        P("fsdp"),
        P("fsdp"),
        P("fsdp"),
        P("fsdp", None),
        P("fsdp"),
        P("fsdp", None),
        P("fsdp"),
    )
    return jax.shard_map(shards, mesh=mesh, in_specs=in_specs, out_specs=out_specs, check_vma=False)
```

profile of v0, /device:TPU:0, one launch (start us, length us, event | category | flops | bytes accessed | tf_op | source)
XLA Modules:
  0.0 5150.6 jit_solution(12142075254592532419)
XLA Ops:
  21.9 13.2 all-gather.22.cloned.1.call-done
  42.1 17.3 all-gather.26.cloned.1.call-done
  103.0 80.3 %all-gather.24.cloned.1.call-done = bf16[8192,768]{1,0:T(8,128)(2,1)} async-done(((bf16[256,768]{1,0:T(8,128)(2,1)}), bf16[8192,768]{1,0:T(8,128)(2,1)}) %all-gather.24.cloned.1.call-update) | async-done | bytes 12582928 | tf_op jit(solution)/shard_map/all_gather | solution.py:257
  183.3 97.6 %all-gather.28.cloned.1.call-done = bf16[8192,768]{1,0:T(8,128)(2,1)} async-done(((bf16[256,768]{1,0:T(8,128)(2,1)}), bf16[8192,768]{1,0:T(8,128)(2,1)}) %all-gather.28.cloned.1.call-update) | async-done | bytes 12582928 | tf_op jit(solution)/shard_map/all_gather | solution.py:258
  293.4 991.9 %while.143 = (s32[]{:T(128)}, bf16[2,33,128,768]{3,2,1,0:T(8,128)(2,1)}, bf16[2,33,128,768]{3,2,1,0:T(8,128)(2,1)}, s32[64]{0:T(128)S(1)}, s32[2]{0:T(128)S(1)},...) while((s32[]{:T(128)}, ...), condition=%wide.region_5.6_spmd, body=%wide.region_2.5_spmd.sunk | while | flops 786506 | bytes 3937191 | solution.py:82
  1285.3 18.3 fusion.189
  1304.8 112.1 %while.147 = (s32[]{:T(128)}, bf16[12,128,64]{1,2,0:T(8,128)(2,1)S(1)}, f32[12,128]{1,0:T(8,128)}, f32[12,128]{1,0:T(8,128)}, s32[12]{0:T(128)S(1)}, /*index=5*/...) while((s32[]{:T(128)}, ...), condition=%wide.region_18.19_spmd.clone, body=%wide.region_15.18_spmd.clone.sunk | while | flops 145981184 | bytes 8795399 | solution.py:99
  1417.6 81.5 %while.146 = (s32[]{:T(128)}, bf16[12,128,64]{1,2,0:T(8,128)(2,1)S(1)}, f32[12,128]{1,0:T(8,128)S(1)}, f32[12,128]{1,0:T(8,128)S(1)}, s32[12]{0:T(128)S(1)}, /*i...) while((s32[]{:T(128)}, ...), condition=%wide.region_12.13_spmd.clone, body=%wide.region_9.12_spmd.clone.sunk | while | flops 145981184 | bytes 8795399 | solution.py:99
  1524.9 155.8 %while.149 = (s32[]{:T(128)}, bf16[12,128,64]{1,2,0:T(8,128)(2,1)S(1)}, f32[12,128]{1,0:T(8,128)}, s32[12]{0:T(128)}, bf16[128,768]{1,0:T(8,128)(2,1)}, /*index=...) while((s32[]{:T(128)}, ...), condition=%wide.region_28.29_spmd.clone, body=%wide.region_26.28_spmd.clone.sunk | while | flops 215728000 | bytes 14236481 | solution.py:120
  1682.5 163.1 %while.148 = (s32[]{:T(128)}, bf16[12,128,64]{1,2,0:T(8,128)(2,1)}, f32[12,128]{1,0:T(8,128)}, s32[12]{0:T(128)}, bf16[128,768]{1,0:T(8,128)(2,1)}, /*index=5*/b...) while((s32[]{:T(128)}, bf16[12,128,64]{1,2,0:T(8,128)(2,1)}, ...), condition=%wide.region_25.26_spmd.clone, body=%wide.region_23.25_spmd.clone.sunk | while | flops 215728000 | bytes 14236481 | solution.py:120
  1845.7 76.6 %all_gather.85 = f32[12,8192]{1,0:T(8,128)} all-gather(f32[12,256]{1,0:T(8,128)} %pad_maximum_fusion.9), channel_id=1, replica_groups=mesh['ctx'=16,'fsdp'=2] {'ctx','fsdp'}, dimensions={1}, use_global_device_ids=true | all-gather | bytes 405504 | tf_op jit(solution)/shard_map/all_gather | solution.py:344
  1922.3 72.4 %all_gather.86 = f32[12,8192]{1,0:T(8,128)} all-gather(f32[12,256]{1,0:T(8,128)} %pad_maximum_fusion.10), channel_id=1, replica_groups=mesh['ctx'=16,'fsdp'=2] {'ctx','fsdp'}, dimensions={1}, use_global_device_ids=true | all-gather | bytes 405504 | tf_op jit(solution)/shard_map/all_gather | solution.py:345
  1995.5 73.2 %all_gather.87 = f32[12,8192]{1,0:T(8,128)} all-gather(f32[12,256]{1,0:T(8,128)S(1)} %pad_maximum_fusion.11), channel_id=1, replica_groups=mesh['ctx'=16,'fsdp'=2] {'ctx','fsdp'}, dimensions={1}, use_global_device_ids=true | all-gather | bytes 405504 | tf_op jit(solution)/shard_map/all_gather | solution.py:346
  2068.8 710.4 %while.145 = (s32[]{:T(128)}, f32[2,33,12,128]{3,2,1,0:T(8,128)S(1)}, f32[2,33,12,128]{3,2,1,0:T(8,128)S(1)}, f32[2,33,12,128]{3,2,1,0:T(8,128)S(1)}, s32[64]{0:...) while((s32[]{:T(128)}, ...), condition=%wide.region_37.38_spmd, body=%wide.region_34.37_spmd.sunk | while | flops 18504 | bytes 209357 | solution.py:82
  2810.8 991.2 %while.144 = (s32[]{:T(128)}, bf16[2,33,128,768]{3,2,1,0:T(8,128)(2,1)}, bf16[2,33,128,768]{3,2,1,0:T(8,128)(2,1)}, s32[64]{0:T(128)S(1)}, s32[2]{0:T(128)S(1)},...) while((s32[]{:T(128)}, ...), condition=%wide.region_32.33_spmd, body=%wide.region_29.32_spmd.sunk | while | flops 786504 | bytes 3937167 | solution.py:82
  3802.0 10.9 fusion.188
  3821.3 249.6 %while.151 = (s32[]{:T(128)}, bf16[12,128,64]{1,2,0:T(8,128)(2,1)}, bf16[12,128,64]{1,2,0:T(8,128)(2,1)S(1)}, s32[12]{0:T(128)}, bf16[4224,768]{1,0:T(8,128)(2,1...) while((s32[]{:T(128)}, bf16[12,128,64]{1,2,0:T(8,128)(2,1)}, ...), condition=%wide.region_42.43_spmd.clone, body=%wide.region_41.42_spmd.clone.sunk | while | flops 284934144 | bytes 11178577 | solution.py:145
  4072.4 243.6 %while.150 = (s32[]{:T(128)}, bf16[12,128,64]{1,2,0:T(8,128)(2,1)}, bf16[12,128,64]{1,2,0:T(8,128)(2,1)S(1)}, s32[12]{0:T(128)}, bf16[4224,768]{1,0:T(8,128)(2,1...) while((s32[]{:T(128)}, bf16[12,128,64]{1,2,0:T(8,128)(2,1)}, ...), condition=%wide.region_39.40_spmd.clone, body=%wide.region_38.39_spmd.clone.sunk | while | flops 284934144 | bytes 11179857 | solution.py:145
  4325.4 585.0 %all-reduce.12 = (bf16[768]{0:T(1024)(128)(2,1)S(1)}, bf16[768]{0:T(1024)(128)(2,1)S(1)}, bf16[768,768]{1,0:T(8,128)(2,1)}, bf16[768]{0:T(1024)(128)(2,1)S(1)}, ...) all-reduce(f32[768]{0:T(1024)S(1)} %get-tuple-element.1378, ...), channel_id=1, replica_groups=mesh['ctx'=16,'fsdp'=2] {'ctx'}, use_global_device_ids=true, to_apply=%region_46.47 | all-reduce | flops 7087104 | bytes 42522624 | tf_op jit(solution)/shard_map/psum | solution.py:397
  4944.7 21.7 reduce-scatter.9.cloned.1.call-done
  4968.5 21.9 reduce-scatter.11.cloned.1.call-done
  4992.5 21.8 reduce-scatter.13.cloned.1.call-done
  5016.5 60.6 %reduce-scatter.15.cloned.1.call-done = bf16[384,3072]{1,0:T(8,128)(2,1)} async-done(((bf16[768,3072]{1,0:T(8,128)(2,1)}), bf16[384,3072]{1,0:T(8,128)(2,1)}) %reduce-scatter.15.cloned.1.call-update) | async-done | bytes 2359312 | tf_op jit(solution)/shard_map/reduce_scatter | solution.py:451
  5081.5 57.9 %reduce-scatter.17.cloned.1.call-done = bf16[1536,768]{1,0:T(8,128)(2,1)} async-done(((bf16[3072,768]{1,0:T(8,128)(2,1)}), bf16[1536,768]{1,0:T(8,128)(2,1)}) %reduce-scatter.17.cloned.1.call-update) | async-done | bytes 2359312 | tf_op jit(solution)/shard_map/reduce_scatter | solution.py:457
  (2979 shorter events, 3255.5 us)
Async XLA Ops:
  7.2 27.9 all-gather.22.cloned.1.call-start
  7.9 51.5 %all-gather.26.cloned.1.call-start = ((), (), s32[]{:S(2)}) async-start(), calls=%async_computation.9 | async-start | bytes 1769472 | tf_op jit(solution)/shard_map/all_gather | solution.py:176
  8.7 91.1 %all-gather.20.cloned.1.call-start = ((), (), s32[]{:S(2)}) async-start(), calls=%async_computation.6 | async-start | bytes 1769472 | tf_op jit(solution)/shard_map/all_gather | solution.py:173
  9.4 173.9 %all-gather.24.cloned.1.call-start = ((), (), s32[]{:S(2)}) async-start(), calls=%async_computation.8 | async-start | bytes 12976128 | tf_op jit(solution)/shard_map/all_gather | solution.py:257
  37.7 243.2 %all-gather.28.cloned.1.call-start = ((), (), s32[]{:S(2)}) async-start(), calls=%async_computation.10 | async-start | bytes 12976128 | tf_op jit(solution)/shard_map/all_gather | solution.py:258
  62.0 1437.1 %all-gather.30.cloned.1.call-start = ((), (), s32[]{:S(2)}) async-start(), calls=%async_computation.11 | async-start | bytes 1769472 | tf_op jit(solution)/shard_map/all_gather | solution.py:178
  62.7 1439.2 %all-gather.32.cloned.1.call-start = ((), (), s32[]{:S(2)}) async-start(), calls=%async_computation.12 | async-start | bytes 7077888 | tf_op jit(solution)/shard_map/all_gather | solution.py:182
  63.5 1444.7 %all-gather.34.cloned.1.call-start = ((), (), s32[]{:S(2)}) async-start(), calls=%async_computation.13 | async-start | bytes 7077888 | tf_op jit(solution)/shard_map/all_gather | solution.py:184
  64.2 2734.0 %all-gather.36.cloned.1.call-start = ((), (), s32[]{:S(2)}) async-start(), calls=%async_computation.14 | async-start | bytes 12976128 | tf_op jit(solution)/shard_map/all_gather | solution.py:329
  90.3 1411.6 %copy-start.38 = (f32[768]{0:T(1024)}, f32[768]{0:T(1024)S(1)}, u32[]{:S(2)}) copy-start(f32[768]{0:T(1024)S(1)} %reshape.1608) | copy-start | bytes 9220
  102.5 2695.8 %all-gather.38.cloned.1.call-start = ((), (), s32[]{:S(2)}) async-start(), calls=%async_computation.15 | async-start | bytes 12976128 | tf_op jit(solution)/shard_map/all_gather | solution.py:330
  1845.7 3096.8 %reduce-scatter.7.cloned.1.call-start = ((), (), s32[]{:S(2)}) async-start(), calls=%async_computation.16 | async-start | bytes 1769472 | tf_op jit(solution)/shard_map/reduce_scatter | solution.py:424
  1994.7 784.5 %copy-start.11 = (bf16[12,128,64]{1,2,0:T(8,128)(2,1)S(1)}, bf16[12,128,64]{1,2,0:T(8,128)(2,1)}, u32[]{:S(2)}) copy-start(bf16[12,128,64]{1,2,0:T(8,128)(2,1)} %get-tuple-element.1077) | copy-start | bytes 589828
  1994.7 784.5 %copy-start.32 = (f32[768]{0:T(1024)S(1)}, f32[768]{0:T(1024)}, u32[]{:S(2)}) copy-start(f32[768]{0:T(1024)} %copy-done.31) | copy-start | bytes 9220
  1994.8 784.5 %copy-start.47 = (f32[256]{0:T(256)S(1)}, f32[256]{0:T(256)}, u32[]{:S(2)}) copy-start(f32[256]{0:T(256)} %copy-done.46) | copy-start | bytes 3076
  1994.8 784.5 %copy-start.50 = (f32[768]{0:T(1024)S(1)}, f32[768]{0:T(1024)}, u32[]{:S(2)}) copy-start(f32[768]{0:T(1024)} %copy-done.49) | copy-start | bytes 9220
  1994.8 784.5 %copy-start.55 = (f32[256]{0:T(256)S(1)}, f32[256]{0:T(256)}, u32[]{:S(2)}) copy-start(f32[256]{0:T(256)} %copy-done.54) | copy-start | bytes 3076
  4072.4 243.7 %copy-start.48 = (f32[256]{0:T(256)S(1)}, f32[256]{0:T(256)}, u32[]{:S(2)}) copy-start(f32[256]{0:T(256)} %copy-done.46) | copy-start | bytes 3076
  4072.4 243.7 %copy-start.51 = (f32[768]{0:T(1024)S(1)}, f32[768]{0:T(1024)}, u32[]{:S(2)}) copy-start(f32[768]{0:T(1024)} %copy-done.49) | copy-start | bytes 9220
  4910.5 55.9 %reduce-scatter.9.cloned.1.call-start = ((), (), s32[]{:S(2)}) async-start(), calls=%async_computation.17 | async-start | bytes 1769472 | tf_op jit(solution)/shard_map/reduce_scatter | solution.py:430
  4911.1 79.3 %reduce-scatter.11.cloned.1.call-start = ((), (), s32[]{:S(2)}) async-start(), calls=%async_computation.18 | async-start | bytes 1769472 | tf_op jit(solution)/shard_map/reduce_scatter | solution.py:433
  4911.8 102.5 %reduce-scatter.13.cloned.1.call-start = ((), (), s32[]{:S(2)}) async-start(), calls=%async_computation.19 | async-start | bytes 1769472 | tf_op jit(solution)/shard_map/reduce_scatter | solution.py:439
  4912.4 164.7 %reduce-scatter.15.cloned.1.call-start = ((), (), s32[]{:S(2)}) async-start(), calls=%async_computation.20 | async-start | bytes 7077888 | tf_op jit(solution)/shard_map/reduce_scatter | solution.py:451
  4913.0 226.4 %reduce-scatter.17.cloned.1.call-start = ((), (), s32[]{:S(2)}) async-start(), calls=%async_computation.21 | async-start | bytes 7077888 | tf_op jit(solution)/shard_map/reduce_scatter | solution.py:457
  (82 other events, 1404.3 us)
Sparse Core Ops, SparseCore 0:
  9.6 25.4 all-gather.21
  36.6 22.7 all-gather.25
  61.0 22.8 all-gather.19
  87.2 96.0 all-gather.23
  186.6 94.2 all-gather.27
  282.3 21.0 all-gather.29
  304.9 62.6 all-gather.31
  369.1 62.6 all-gather.33
  435.3 96.0 all-gather.35
  1845.8 101.2 all-gather.37
  4910.6 31.1 reduce-scatter.6
  4944.6 21.7 reduce-scatter.8
  4968.6 21.7 reduce-scatter.10
  4992.6 21.7 reduce-scatter.12
  5017.1 59.9 reduce-scatter.14
  5079.4 59.9 reduce-scatter.16
where the time goes:
time: 5220 us; the launch traced here: 5150 us
  other arithmetic  1530 us (29%)
  local copies, waits for them, and re-layouts  1020 us (20%)
  blocking collectives  859 us (16%)
  matrix products  673 us (13%)
  loops' own time  648 us (12%)
  waiting for transfers between devices  399 us (8%)
    scatter x704, other arithmetic, take(): held[member].at[index, spot].set(jnp.where(inside, fresh, current))  1340 us
    psum x1, blocking collectives, shards(): lax.psum((terms[0], terms[1], terms[2], terms[3], terms[4], terms[5], ter...  585 us
    another operation x3, loops' own time, make_collect(): return lax.fori_loop(0, blocks_here, take, carry)  506 us
    dynamic_slice x896, local copies, waits for them, and re-layouts, take(): current = held[member][index, spot]  484 us
    dot_general x102, matrix products, inner(): lax.dot_general(left, right, (((1,), (1,)), ((), ())), preferred_element_...  359 us
    dot_general x54, matrix products, outer(): lax.dot_general(left, right, (((0,), (0,)), ((), ())), preferred_element_...  173 us
    another operation x193, other arithmetic  138 us
    dynamic_slice x192, local copies, waits for them, and re-layouts, take(): label = lax.dynamic_index_in_dim(deal, number, keepdims=False)  112 us
  transfers between devices with their start and end apart: 16, of which 9 were waited for; matrix products, arithmetic and copies ran while one was open for 37% of the time, Pallas kernels for 0%

commit v1 on v0

v1 whole, which is shorter than its diff:
```python
import functools

import jax
import jax.numpy as jnp
from jax import lax
from jax.experimental import pallas as pl
from jax.experimental.pallas import tpu as pltpu
from jax.sharding import Mesh
from jax.sharding import PartitionSpec as P

HEADS = 12
DH = 64
NSUM = 50
SEG = 2048
BLK = 128
GROUPS = 4
PER = HEADS // GROUPS
HW = PER * DH
WIDE = PER * BLK
CHUNK = 2 * BLK
EPS = 1e-05
SCALE = 0.125
MASKED = -1e30
ROOT_HALF = 0.7071067811865476
VMEM_LIMIT = 56 << 20
bf16 = jnp.bfloat16
f32 = jnp.float32


def smooth_unit(values):
    return 0.5 * values * (1.0 + jax.scipy.special.erf(values * ROOT_HALF))


def layer_norm(values, gain, shift):
    mean = jnp.mean(values, axis=-1, keepdims=True)
    centred = values - mean
    spread = jnp.mean(centred * centred, axis=-1, keepdims=True)
    return centred * lax.rsqrt(spread + EPS) * gain + shift


def outer(left, right):
    return lax.dot_general(left, right, (((0,), (0,)), ((), ())), preferred_element_type=f32)


def inner(left, right):
    return lax.dot_general(left, right, (((1,), (1,)), ((), ())), preferred_element_type=f32)


def dot(left, right):
    return jnp.dot(left, right, preferred_element_type=f32)


def first_visible(positions, doc_lengths):
    count = doc_lengths.shape[0]
    order = jnp.arange(count)
    starts = jnp.sum(jnp.where(order[None, :] < order[:, None], doc_lengths[None, :], 0), axis=1)
    before = starts <= positions[..., None]
    begin = jnp.max(jnp.where(before, starts, 0), axis=-1)
    return jnp.where(positions - begin >= SEG + NSUM, begin + SEG, begin)


def spread_heads_t(part_t, order):
    rows = []
    zero = jnp.zeros((DH, BLK), part_t.dtype)
    for head in order:
        if head is None:
            rows.append(jnp.zeros((DH, WIDE), part_t.dtype))
        else:
            piece = part_t[DH * head : DH * head + DH]
            rows.append(
                jnp.concatenate([piece if h == head else zero for h in range(PER)], axis=1)
            )
    return jnp.concatenate(rows, axis=0)


K_ORDER = (0, 1, 2, None)
V_ORDER = (None, 2, 0, 1)


def visible(chunk, first, own):
    at = chunk * CHUNK + lax.broadcasted_iota(jnp.int32, (CHUNK, BLK), 0)
    allowed = (at >= first) & (at <= own)
    return jnp.concatenate([allowed] * PER, axis=1)


def load_chunk(kv_ref, where_ref, chunk):
    return jnp.concatenate(
        [kv_ref[where_ref[2 * chunk]], kv_ref[where_ref[2 * chunk + 1]]], axis=0
    )


def forward_kernel(
    where_ref, text_ref, low_ref, high_ref, q_ref, kv_ref, first_ref,
    out_ref, wide_ref, lse_ref, vt_ref, acc_ref,
):
    chunks = kv_ref.shape[0] // 2

    def turn(chunk, _):
        vt_ref[chunk] = load_chunk(kv_ref, where_ref, chunk)[:, BLK : 3 * BLK].T[DH:]
        return _

    lax.fori_loop(0, chunks, turn, 0)

    def one_slot(slot, _):
        wide_q = spread_heads_t(q_ref[slot].T[:HW], K_ORDER)
        first = first_ref[slot]
        own = text_ref[slot] * BLK + lax.broadcasted_iota(jnp.int32, (1, BLK), 1)
        acc_ref[...] = jnp.zeros_like(acc_ref)

        def step(chunk, carry):
            top, total = carry
            part = load_chunk(kv_ref, where_ref, chunk)
            scores = dot(part[:, : 2 * BLK], wide_q)
            scores = jnp.where(visible(chunk, first, own), scores, MASKED)
            fresh = jnp.maximum(top, jnp.max(scores, axis=0, keepdims=True))
            expo = jnp.exp(scores - fresh)
            shrink = jnp.exp(top - fresh)
            total = total * shrink + jnp.sum(expo, axis=0, keepdims=True)
            acc_ref[...] = acc_ref[...] * shrink + dot(vt_ref[chunk], expo.astype(bf16))
            return fresh, total

        top, total = lax.fori_loop(
            low_ref[slot],
            high_ref[slot] + 1,
            step,
            (jnp.full((1, WIDE), MASKED, f32), jnp.zeros((1, WIDE), f32)),
        )
        lse_ref[slot] = top + jnp.log(total)
        scaled = acc_ref[...] / total
        pieces = []
        for head in range(PER):
            row = DH * V_ORDER.index(head) - DH
            pieces.append(scaled[row : row + DH, BLK * head : BLK * head + BLK])
        kept = jnp.concatenate(pieces, axis=0)
        wide_ref[slot] = kept
        out_ref[slot] = kept.astype(bf16)
        return _

    lax.fori_loop(0, q_ref.shape[0], one_slot, 0)


def whole_vmem():
    return pl.BlockSpec(memory_space=pltpu.VMEM)


def whole_smem():
    return pl.BlockSpec(memory_space=pltpu.SMEM)


def attend_forward(where, text, low, high, q, kv, first):
    slots = q.shape[0]
    blocks = kv.shape[0]
    return pl.pallas_call(
        forward_kernel,
        out_shape=(
            jax.ShapeDtypeStruct((slots, HW, BLK), bf16),
            jax.ShapeDtypeStruct((slots, HW, BLK), f32),
            jax.ShapeDtypeStruct((slots, 1, WIDE), f32),
        ),
        in_specs=[whole_smem()] * 4 + [whole_vmem()] * 3,
        out_specs=(whole_vmem(),) * 3,
        scratch_shapes=[
            pltpu.VMEM((blocks // 2, HW, CHUNK), bf16),
            pltpu.VMEM((HW, WIDE), f32),
        ],
        compiler_params=pltpu.CompilerParams(vmem_limit_bytes=VMEM_LIMIT),
        name="attend_forward",
    )(where, text, low, high, q, kv, first)


def backward_kernel(
    where_ref, text_ref, low_ref, high_ref, q_ref, kv_ref, first_ref, lse_ref, do_ref, wide_ref,
    dq_ref, dkv_ref, qt_ref, qm_ref, dot_ref, dom_ref, delta_ref, acc_ref, dk_acc, dv_acc,
):
    slots = q_ref.shape[0]
    chunks = kv_ref.shape[0] // 2

    def ready(slot, _):
        q = q_ref[slot]
        qt_ref[slot] = spread_heads_t(q.T[:HW], K_ORDER)
        lane = lax.broadcasted_iota(jnp.int32, (BLK, 2 * BLK), 1) // DH
        zero = jnp.zeros_like(q)
        qm_ref[slot] = jnp.concatenate(
            [jnp.where(lane == K_ORDER.index(h), q, zero) for h in range(PER)], axis=0
        )
        grad_t = do_ref[slot]
        dot_ref[slot] = spread_heads_t(grad_t, V_ORDER)
        ordered = jnp.concatenate(
            [
                jnp.zeros((DH, BLK), bf16) if h is None else grad_t[DH * h : DH * h + DH]
                for h in V_ORDER
            ],
            axis=0,
        ).T
        dom_ref[slot] = jnp.concatenate(
            [jnp.where(lane == V_ORDER.index(h), ordered, zero) for h in range(PER)], axis=0
        )
        both = grad_t.astype(f32) * wide_ref[slot]
        delta_ref[slot] = jnp.concatenate(
            [jnp.sum(both[DH * h : DH * h + DH], axis=0, keepdims=True) for h in range(PER)],
            axis=1,
        )
        acc_ref[slot] = jnp.zeros((HW, WIDE), f32)
        return _

    lax.fori_loop(0, slots, ready, 0)

    def one_chunk(chunk, _):
        part = load_chunk(kv_ref, where_ref, chunk)
        keys = part[:, : 2 * BLK]
        vals = part[:, BLK:]
        keys_t = keys.T[:HW]
        dk_acc[...] = jnp.zeros_like(dk_acc)
        dv_acc[...] = jnp.zeros_like(dv_acc)

        def one_slot(slot, kept):
            @pl.when((low_ref[slot] <= chunk) & (chunk <= high_ref[slot]))
            def _():
                own = text_ref[slot] * BLK + lax.broadcasted_iota(jnp.int32, (1, BLK), 1)
                scores = dot(keys, qt_ref[slot])
                probs = jnp.where(
                    visible(chunk, first_ref[slot], own), jnp.exp(scores - lse_ref[slot]), 0.0
                )
                dprobs = dot(vals, dot_ref[slot])
                dscores = (probs * (dprobs - delta_ref[slot])).astype(bf16)
                dv_acc[...] += dot(probs.astype(bf16), dom_ref[slot])
                dk_acc[...] += dot(dscores, qm_ref[slot])
                acc_ref[slot] += dot(keys_t, dscores)

            return kept

        lax.fori_loop(0, slots, one_slot, 0)
        packed = jnp.concatenate(
            [
                dk_acc[:, :BLK],
                dk_acc[:, BLK:] + dv_acc[:, :BLK],
                dv_acc[:, BLK:],
            ],
            axis=1,
        ).astype(bf16)
        dkv_ref[where_ref[2 * chunk]] = packed[:BLK]
        dkv_ref[where_ref[2 * chunk + 1]] = packed[BLK:]
        return _

    lax.fori_loop(0, chunks, one_chunk, 0)

    def finish(slot, _):
        total = acc_ref[slot]
        kept = jnp.concatenate(
            [total[DH * h : DH * h + DH, BLK * h : BLK * h + BLK] for h in range(PER)]
            + [jnp.zeros((DH, BLK), f32)],
            axis=0,
        )
        dq_ref[slot] = kept.T.astype(bf16)
        return _

    lax.fori_loop(0, slots, finish, 0)


def attend_backward(where, text, low, high, q, kv, first, lse, grad_t, wide):
    slots = q.shape[0]
    return pl.pallas_call(
        backward_kernel,
        out_shape=(
            jax.ShapeDtypeStruct((slots, BLK, 2 * BLK), bf16),
            jax.ShapeDtypeStruct(kv.shape, bf16),
        ),
        in_specs=[whole_smem()] * 4 + [whole_vmem()] * 6,
        out_specs=(whole_vmem(),) * 2,
        scratch_shapes=[
            pltpu.VMEM((slots, 2 * BLK, WIDE), bf16),
            pltpu.VMEM((slots, WIDE, 2 * BLK), bf16),
            pltpu.VMEM((slots, 2 * BLK, WIDE), bf16),
            pltpu.VMEM((slots, WIDE, 2 * BLK), bf16),
            pltpu.VMEM((slots, 1, WIDE), f32),
            pltpu.VMEM((slots, HW, WIDE), f32),
            pltpu.VMEM((CHUNK, 2 * BLK), f32),
            pltpu.VMEM((CHUNK, 2 * BLK), f32),
        ],
        compiler_params=pltpu.CompilerParams(vmem_limit_bytes=VMEM_LIMIT + (4 << 20)),
        name="attend_backward",
    )(where, text, low, high, q, kv, first, lse, grad_t, wide)


def pack_kv(key_part, value_part):
    return jnp.concatenate(
        [key_part, value_part[..., 2 * DH :], value_part[..., : 2 * DH]], axis=-1
    )


def unpack_kv(both):
    return both[..., :HW], jnp.concatenate([both[..., HW + DH :], both[..., HW : HW + DH]], axis=-1)


ROWS = ("r", "core", "x")
ALL = ("g", "r", "core", "x")


def shards(
    tokens, cotangent, doc_lengths, deal, first_gain, first_shift, query_weight, query_bias,
    key_weight, value_weight, value_bias, output_weight, output_bias, second_gain, second_shift,
    up_weight, up_bias, down_weight, down_bias,
):
    def whole(item):
        return lax.all_gather(item, "x", axis=0, tiled=True)

    rows, width = tokens.shape
    group = lax.axis_index("g")
    rest = lax.axis_index(ROWS)
    blocks = deal.shape[0]
    per_group = blocks // (2 * GROUPS)

    gathered = deal.reshape(GROUPS, per_group, 2).transpose(1, 0, 2).reshape(-1)
    order = jnp.arange(blocks, dtype=jnp.int32)
    where = jnp.sum(jnp.where(gathered[None, :] == order[:, None], order[None, :], 0), axis=1)
    text = lax.dynamic_slice_in_dim(gathered, rest * 2 * GROUPS, 2 * GROUPS)
    positions = text[:, None] * BLK + jnp.arange(BLK, dtype=jnp.int32)[None, :]
    first = first_visible(positions, doc_lengths)
    low = first[:, 0] // CHUNK
    high = text // 2

    def columns(item):
        return lax.dynamic_slice_in_dim(item, group * HW, HW, 1)

    narrow = jnp.concatenate(
        [columns(query_weight), columns(key_weight), columns(value_weight)], axis=1
    )
    narrow = whole(narrow)
    wq, wk, wv = narrow[:, :HW], narrow[:, HW : 2 * HW], narrow[:, 2 * HW :]
    small = whole(
        jnp.stack([first_gain, first_shift, query_bias, value_bias, output_bias, second_gain, second_shift, down_bias], axis=1)
    ).astype(f32)
    lower_gain, lower_shift, query_add, value_add, output_add, upper_gain, upper_shift, reduce_add = (
        small[:, i] for i in range(8)
    )
    query_part = lax.dynamic_slice_in_dim(query_add, group * HW, HW)
    value_part = lax.dynamic_slice_in_dim(value_add, group * HW, HW)
    expand_add = whole(up_bias).astype(f32)
    output_mat = whole(output_weight)
    expand_mat = whole(up_weight)
    reduce_mat = whole(down_weight)

    lined = lax.all_gather(tokens, "g", axis=0, tiled=True).astype(f32)
    normed = layer_norm(lined, lower_gain, lower_shift).astype(bf16)
    q = ((dot(normed, wq) + query_part) * SCALE).astype(bf16)
    k = dot(normed, wk).astype(bf16)
    v = (dot(normed, wv) + value_part).astype(bf16)
    kv = lax.all_gather(pack_kv(k, v), ROWS, axis=0, tiled=True)
    kv = kv.reshape(blocks, BLK, 2 * HW)
    q_pad = jnp.pad(q, ((0, 0), (0, 2 * BLK - HW))).reshape(2 * GROUPS, BLK, 2 * BLK)
    first = first.reshape(2 * GROUPS, 1, BLK)
    out_t, wide, lse = attend_forward(where, text, low, high, q_pad, kv, first)

    def swap(item):
        item = item.reshape(GROUPS, 2, HW, BLK)
        return lax.all_to_all(item, "g", 0, 0, tiled=True)

    attn_t = swap(out_t).transpose(0, 2, 1, 3).reshape(width, rows)

    inputs = tokens.astype(f32)
    middle = inputs + outer(attn_t, output_mat) + output_add
    second_normed = layer_norm(middle, upper_gain, upper_shift).astype(bf16)
    expanded = dot(second_normed, expand_mat) + expand_add
    hidden = smooth_unit(expanded).astype(bf16)
    result = (middle + dot(hidden, reduce_mat) + reduce_add).astype(bf16)
    grad_in = cotangent.astype(f32)
    term_reduce_mat = outer(hidden, cotangent)
    term_reduce_add = jnp.sum(grad_in, axis=0)
    grad_hidden = inner(cotangent, reduce_mat).astype(bf16)
    _, pull_unit = jax.vjp(smooth_unit, expanded)
    grad_expand = pull_unit(grad_hidden.astype(f32))[0].astype(bf16)
    term_expand_mat = outer(second_normed, grad_expand)
    term_expand_add = jnp.sum(grad_expand.astype(f32), axis=0)
    grad_second = inner(grad_expand, expand_mat)
    _, pull_second = jax.vjp(layer_norm, middle, upper_gain, upper_shift)
    grad_middle_part, term_upper_gain, term_upper_shift = pull_second(grad_second)
    grad_middle = grad_in + grad_middle_part
    grad_branch = grad_middle.astype(bf16)
    term_output_mat = dot(attn_t, grad_branch)
    term_output_add = jnp.sum(grad_branch.astype(f32), axis=0)
    grad_mixed_t = inner(output_mat, grad_branch).astype(bf16)

    grad_t = swap(grad_mixed_t.reshape(GROUPS, HW, 2, BLK).transpose(0, 2, 1, 3))
    grad_t = grad_t.reshape(2 * GROUPS, HW, BLK)
    dq, dkv = attend_backward(where, text, low, high, q_pad, kv, first, lse, grad_t, wide)
    dq = dq.reshape(-1, 2 * BLK)[:, :HW] * bf16(SCALE)
    dkv = lax.psum_scatter(dkv.reshape(-1, 2 * HW), ROWS, scatter_dimension=0, tiled=True)
    dk, dv = unpack_kv(dkv)
    grad_first = (inner(dq, wq) + inner(dk, wk) + inner(dv, wv)).astype(bf16)
    grad_first = lax.psum_scatter(grad_first, "g", scatter_dimension=0, tiled=True).astype(f32)
    term_narrow = outer(normed, jnp.concatenate([dq, dk, dv], axis=1)).astype(bf16)
    term_query_add = jnp.sum(dq.astype(f32), axis=0)
    term_value_add = jnp.sum(dv.astype(f32), axis=0)
    _, pull_first = jax.vjp(layer_norm, inputs, lower_gain, lower_shift)
    grad_input_part, term_lower_gain, term_lower_shift = pull_first(grad_first)
    grad_tokens = grad_middle + grad_input_part

    def owned(item, axes):
        mine = lax.psum_scatter(item.astype(bf16), "x", scatter_dimension=0, tiled=True)
        return lax.psum(mine, axes).astype(f32)

    ctx = ("g", "r", "core")
    narrow_own = owned(term_narrow, ("r", "core"))
    narrow_own = lax.all_gather(narrow_own.astype(bf16), "g").astype(f32)
    query_own, key_own, value_own = (
        narrow_own[:, :, i * HW : (i + 1) * HW].transpose(1, 0, 2).reshape(-1, width)
        for i in range(3)
    )
    half = lax.axis_index("x") * (width // 2)

    def own_half(item):
        return lax.dynamic_slice_in_dim(item, half, width // 2)

    vectors = jnp.stack(
        [
            term_lower_gain, term_lower_shift, term_output_add, term_upper_gain, term_upper_shift, term_reduce_add,
            lax.dynamic_update_slice_in_dim(jnp.zeros((width,), f32), term_query_add, group * HW, 0),
            lax.dynamic_update_slice_in_dim(jnp.zeros((width,), f32), term_value_add, group * HW, 0),
        ]
        + [term_expand_add[i * width : (i + 1) * width] for i in range(4)]
    )
    vectors = lax.psum(vectors, ALL)
    expand_own = lax.dynamic_slice_in_dim(
        vectors[8:].reshape(-1), lax.axis_index("x") * (2 * width), 2 * width
    )
    return (
        result,
        grad_tokens,
        own_half(vectors[0]),
        own_half(vectors[1]),
        query_own,
        own_half(vectors[6]),
        key_own,
        value_own,
        own_half(vectors[7]),
        owned(term_output_mat, ctx),
        own_half(vectors[2]),
        own_half(vectors[3]),
        own_half(vectors[4]),
        owned(term_expand_mat, ctx),
        expand_own,
        owned(term_reduce_mat, ctx),
        own_half(vectors[5]),
    )


def solution(mesh):
    devices = mesh.devices
    inner_mesh = Mesh(devices.reshape(GROUPS, devices.shape[0] // (2 * GROUPS), 2, 2), ALL)
    row = P(ALL, None)
    mat = P("x", None)
    vec = P("x")
    in_specs = (
        row, row, P(), P(), vec, vec, mat, vec, mat, mat, vec, mat, vec, vec, vec, mat, vec, mat, vec,
    )
    out_specs = (
        row, row, vec, vec, mat, vec, mat, mat, vec, mat, vec, vec, vec, mat, vec, mat, vec,
    )
    return jax.shard_map(
        shards, mesh=inner_mesh, in_specs=in_specs, out_specs=out_specs, check_vma=False
    )
```

time: 5220 us -> 834 us (0.16); the launches traced: 5150 us -> 833 us
  other arithmetic: 1530 us -> 24.6 us
  local copies, waits for them, and re-layouts: 1020 us -> 50.2 us
  blocking collectives: 859 us -> 81.3 us
  loops' own time: 648 us -> 0 us
  matrix products: 673 us -> 43.5 us
  waiting for transfers between devices: 399 us -> 550 us
  Pallas kernels: 0 us -> 63.8 us
    scatter x704 -> x0, other arithmetic: 1340 us -> none  [take(): held[member].at[index, spot].set(jnp.where(inside, fresh, current))]
    dynamic_slice x1208 -> x12, local copies, waits for them, and re-layouts: 747 us -> 6.95 us  [the longest x8 4.79 us: own_half(): return lax.dynamic_slice_in_dim(item, half, width // 2)]
    another operation x9 -> x0, loops' own time: 648 us -> none  [the longest x3 506 us: make_collect(): return lax.fori_loop(0, blocks_here, take, carry)]
    psum x1, blocking collectives: 585 us -> 42.3 us  [shards(): vectors = lax.psum(vectors, ALL)]
    dot_general x102 -> x6, matrix products: 359 us -> 12.7 us  [inner(): lax.dot_general(left, right, (((1,), (1,)), ((), ())), preferred_element_...]
    all_gather x12 -> x3, blocking collectives: 265 us -> 22.7 us  [whole(): return lax.all_gather(item, 'x', axis=0, tiled=True)]
    dot_general x54 -> x4, matrix products: 173 us -> 15.6 us  [outer(): lax.dot_general(left, right, (((0,), (0,)), ((), ())), preferred_element_...]
    psum x0 -> x2, waiting for transfers between devices: none -> 155 us  [owned(): return lax.psum(mine, axes).astype(f32)]
  transfers between devices with their start and end apart: 16 -> 15, of which waited for: 9 -> 13; matrix products, arithmetic and copies ran while one was open for 37% -> 9% of each run, Pallas kernels for 0% -> 3%
where the time goes in v1:
time: 834 us; the launch traced here: 833 us
  waiting for transfers between devices  550 us (66%)
  blocking collectives  81.3 us (10%)
  Pallas kernels  63.8 us (8%)
  local copies, waits for them, and re-layouts  50.2 us (6%)
  matrix products  43.5 us (5%)
  other arithmetic  24.6 us (3%)
  between operations  14.5 us (2%)
    psum x2, waiting for transfers between devices, owned(): return lax.psum(mine, axes).astype(f32)  155 us
    reduce_scatter x3, waiting for transfers between devices, owned(): lax.psum_scatter(item.astype(bf16), 'x', scatter_dimension=0, tiled=True)  148 us
    all_gather x3, waiting for transfers between devices, whole(): return lax.all_gather(item, 'x', axis=0, tiled=True)  91 us
    reduce_scatter x1, waiting for transfers between devices, shards(): lax.psum_scatter(dkv.reshape(-1, 2 * HW), ROWS, scatter_dimension=0, tile...  59.1 us
    psum x1, blocking collectives, shards(): vectors = lax.psum(vectors, ALL)  42.3 us
    all_gather x1, waiting for transfers between devices, shards(): kv = lax.all_gather(pack_kv(k, v), ROWS, axis=0, tiled=True)  37.7 us
    pallas_call x1, Pallas kernels, attend_backward(): pl.pallas_call(backward_kernel, out_shape=(jax.ShapeDtypeStruct((slots, B...  36.2 us
    reduce_scatter x1, waiting for transfers between devices, shards(): lax.psum_scatter(grad_first, 'g', scatter_dimension=0, tiled=True)  28.5 us
  transfers between devices with their start and end apart: 15, of which 13 were waited for; matrix products, arithmetic and copies ran while one was open for 9% of the time, Pallas kernels for 3%

profile of v1, /device:TPU:0, one launch (start us, length us, event | category | flops | bytes accessed | tf_op | source)
XLA Modules:
  0.0 832.8 jit_solution(7688326787364389364)
XLA Ops:
  13.5 5.2 all_gather.31
  20.5 12.8 %all_gather.32 = bf16[768,576]{1,0:T(8,128)(2,1)S(1)} all-gather(bf16[384,576]{1,0:T(8,128)(2,1)S(1)} %pad_maximum_fusion.2), channel_id=1, replica_groups=mesh['g'=4,'r'=2,'core'=2,'x'=2] {'x'}, dimensions={0}, use_global_device_ids=true | all-gather | bytes 1327104 | tf_op jit(solution)/shard_map/all_gather | solution.py:305
  33.3 16.2 %all-gather.8.cloned.1.call-done = bf16[1024,768]{1,0:T(8,128)(2,1)} async-done(((bf16[256,768]{1,0:T(8,128)(2,1)}), bf16[1024,768]{1,0:T(8,128)(2,1)}) %all-gather.8.cloned.1.call-update) | async-done | bytes 1572880 | tf_op jit(solution)/shard_map/all_gather | solution.py:343
  61.9 37.7 %all-gather.10.cloned.1.call-done = bf16[8192,384]{0,1:T(8,128)(2,1)} async-done(((bf16[1024,384]{0,1:T(8,128)(2,1)}), bf16[8192,384]{0,1:T(8,128)(2,1)}) %all-gather.10.cloned.1.call-update) | async-done | bytes 6291472 | tf_op jit(solution)/shard_map/all_gather | solution.py:348
  99.6 8.7 %copy.63 = bf16[8192,384]{1,0:T(8,128)(2,1)} copy(bf16[8192,384]{0,1:T(8,128)(2,1)} %all-gather.10.cloned.1.call-done) | data formatting | bytes 12582912 | tf_op jit(solution)/shard_map/all_gather | solution.py:348
  108.3 27.6 %attend_forward.1 = (bf16[8,192,128]{2,1,0:T(8,128)(2,1)}, f32[8,192,128]{2,1,0:T(8,128)}, f32[8,1,384]{2,1,0:T(1,128)}) custom-call(s32[64]{0:T(128)} %select_reduce_fusion.where_ref, s32[8]{0:T(128)} %copy-done.24, s32[8]{0:T(128)} %and_select_fusion.1.low_ref, s32[8]{0:T(128)} %get-tuple-element.116.high_ref, bf16[8,128,256]{2,1,0:T(8,128)(2,1)} %bitcast.64, ...), custom_call_target="tpu_custom_call" | custom-call | tf_op jit(solution)/shard_map/attend_forward/pallas_call | solution.py:153
  154.7 33.5 %all-gather.14.cloned.1.call-done = bf16[768,3072]{1,0:T(8,128)(2,1)} async-done(((bf16[384,3072]{1,0:T(8,128)(2,1)}), bf16[768,3072]{1,0:T(8,128)(2,1)}) %all-gather.14.cloned.1.call-update) | async-done | bytes 4718608 | tf_op jit(solution)/shard_map/all_gather | solution.py:305
  188.2 6.7 multiply_convert_fusion
  194.9 57.4 %all-gather.16.cloned.1.call-done = bf16[3072,768]{1,0:T(8,128)(2,1)} async-done(((bf16[1536,768]{1,0:T(8,128)(2,1)}), bf16[3072,768]{1,0:T(8,128)(2,1)}) %all-gather.16.cloned.1.call-update) | async-done | bytes 4718608 | tf_op jit(solution)/shard_map/all_gather | solution.py:305
  252.3 6.6 convert_reduce_fusion.1
  267.9 16.3 %all_to_all.10 = bf16[4,2,192,128]{3,1,2,0:T(2,128)(2,1)S(1)} all-to-all(bf16[4,2,192,128]{3,1,2,0:T(2,128)(2,1)} %bitcast.68), channel_id=1, replica_groups=mesh['g'=4,'r'=2,'core'=2,'x'=2] {'g'}, dimensions={0} | all-to-all | bytes 786432 | tf_op jit(solution)/shard_map/all_to_all | solution.py:356
  285.0 36.2 %attend_backward.1 = (bf16[8,128,256]{2,1,0:T(8,128)(2,1)}, bf16[64,128,384]{2,1,0:T(8,128)(2,1)}) custom-call(s32[64]{0:T(128)} %select_reduce_fusion.where_ref, s32[8]{0:T(128)} %copy-done.24, s32[8]{0:T(128)} %and_select_fusion.1.low_ref, s32[8]{0:T(128)} %get-tuple-element.116.high_ref, bf16[8,128,256]{2,1,0:T(8,128)(2,1)} %bitcast.65, ...), custom_call_target="tpu_custom_call" | custom-call | tf_op jit(solution)/shard_map/attend_backward/pallas_call | solution.py:262
  323.1 59.1 %reduce-scatter.9.cloned.1.call-done = bf16[1024,384]{1,0:T(8,128)(2,1)} async-done(((bf16[8192,384]{1,0:T(8,128)(2,1)}), bf16[1024,384]{1,0:T(8,128)(2,1)}) %reduce-scatter.9.cloned.1.call-update) | async-done | bytes 786448 | tf_op jit(solution)/shard_map/reduce_scatter | solution.py:387
  392.9 5.2 convolution_convert_fusion.1
  398.4 5.0 convolution_convert_fusion
  403.5 7.5 reduce-scatter.19.cloned.1.call-done
  413.1 22.5 %reduce-scatter.13.cloned.1.call-done = bf16[384,768]{1,0:T(8,128)(2,1)} async-done(((bf16[768,768]{1,0:T(8,128)(2,1)}), bf16[384,768]{1,0:T(8,128)(2,1)}) %reduce-scatter.13.cloned.1.call-update) | async-done | bytes 589840 | tf_op jit(solution)/shard_map/reduce_scatter | solution.py:399
  435.6 63.0 %reduce-scatter.15.cloned.1.call-done = bf16[384,3072]{1,0:T(8,128)(2,1)} async-done(((bf16[768,3072]{1,0:T(8,128)(2,1)}), bf16[384,3072]{1,0:T(8,128)(2,1)}) %reduce-scatter.15.cloned.1.call-update) | async-done | bytes 2359312 | tf_op jit(solution)/shard_map/reduce_scatter | solution.py:399
  498.6 62.8 %reduce-scatter.17.cloned.1.call-done = bf16[1536,768]{1,0:T(8,128)(2,1)} async-done(((bf16[3072,768]{1,0:T(8,128)(2,1)}), bf16[1536,768]{1,0:T(8,128)(2,1)}) %reduce-scatter.17.cloned.1.call-update) | async-done | bytes 2359312 | tf_op jit(solution)/shard_map/reduce_scatter | solution.py:399
  566.5 30.7 %all-reduce.5.cloned.1.call-done = bf16[1,384,576]{1,2,0:T(8,128)(2,1)} async-done(((bf16[1,384,576]{1,2,0:T(8,128)(2,1)}), bf16[1,384,576]{1,2,0:T(8,128)(2,1)}) %all-reduce.5.cloned.1.call-update) | async-done | bytes 442384 | tf_op jit(solution)/shard_map/psum | solution.py:400
  597.5 5.0 fusion.22
  603.2 123.9 %all-reduce.7.cloned.1.call-done = (bf16[384,768]{1,0:T(8,128)(2,1)}, bf16[384,3072]{1,0:T(8,128)(2,1)}, bf16[1536,768]{1,0:T(8,128)(2,1)}) async-done(((bf16[384,768]{1,0:T(8,128)(2,1)}, bf16[384,3072]{1,0:T(8,128)(2,1)}, bf16[1536,768]{1,0:T(8,128)(2,1)}), (bf16[384,768]{1,0:T(8,128)(2,1)}, bf16[384,3072]{1,0:T(8,128)(2,1)}, bf16[1536,768]{1,0:T(8,128)(2,1)})) %all-reduce.7.cloned.1.call-update) | async-done | bytes 5308432 | tf_op jit(solution)/shard_map/psum | solution.py:400
  736.4 28.5 %reduce-scatter.11.cloned.1.call-done = bf16[256,768]{1,0:T(8,128)(2,1)} async-done(((bf16[1024,768]{1,0:T(8,128)(2,1)}), bf16[256,768]{1,0:T(8,128)(2,1)}) %reduce-scatter.11.cloned.1.call-update) | async-done | bytes 393232 | tf_op jit(solution)/shard_map/reduce_scatter | solution.py:390
  770.2 42.3 %psum.35 = f32[12,768]{1,0:T(8,128)S(1)} all-reduce(f32[12,768]{1,0:T(8,128)S(1)} %stack.78), channel_id=1, replica_groups=mesh['g'=4,'r'=2,'core'=2,'x'=2] {'g','r','core','x'}, use_global_device_ids=true, to_apply=%region_24.25 | all-reduce | flops 9216 | bytes 73728 | tf_op jit(solution)/shard_map/psum | solution.py:422
  (204 shorter events, 97.8 us)
Async XLA Ops:
  7.2 11.6 %copy-start = (bf16[384,768]{1,0:T(8,128)(2,1)S(1)}, bf16[384,768]{1,0:T(8,128)(2,1)}, u32[]{:S(2)}) copy-start(bf16[384,768]{1,0:T(8,128)(2,1)} %param.25) | copy-start | bytes 1769476
  7.2 42.2 %all-gather.8.cloned.1.call-start = ((), (), s32[]{:S(2)}) async-start(), calls=%async_computation.8 | async-start | bytes 1966080 | tf_op jit(solution)/shard_map/all_gather | solution.py:343
  7.9 91.7 %all-gather.10.cloned.1.call-start = ((), (), s32[]{:S(2)}) async-start(), calls=%async_computation.9 | async-start | bytes 7077888 | tf_op jit(solution)/shard_map/all_gather | solution.py:348
  55.1 92.2 %all-gather.12.cloned.1.call-start = ((), (), s32[]{:S(2)}) async-start(), calls=%async_computation.10 | async-start | bytes 1769472 | tf_op jit(solution)/shard_map/all_gather | solution.py:305
  55.8 132.4 %all-gather.14.cloned.1.call-start = ((), (), s32[]{:S(2)}) async-start(), calls=%async_computation.11 | async-start | bytes 7077888 | tf_op jit(solution)/shard_map/all_gather | solution.py:305
  56.4 195.9 %all-gather.16.cloned.1.call-start = ((), (), s32[]{:S(2)}) async-start(), calls=%async_computation.12 | async-start | bytes 7077888 | tf_op jit(solution)/shard_map/all_gather | solution.py:305
  57.8 50.5 %copy-start.24 = (s32[8]{0:T(128)}, s32[8]{0:T(128)S(1)}, u32[]{:S(2)}) copy-start(s32[8]{0:T(128)S(1)} %get-tuple-element.117.text_ref) | copy-start | bytes 100
  108.3 34.3 %copy-start.25 = (bf16[1536]{0:T(1024)(128)(2,1)S(1)}, bf16[1536]{0:T(1024)(128)(2,1)}, u32[]{:S(2)}) copy-start(bf16[1536]{0:T(1024)(128)(2,1)} %param.35) | copy-start | bytes 9220
  108.3 43.2 %copy-start.3 = (bf16[256,768]{1,0:T(8,128)(2,1)S(1)}, bf16[256,768]{1,0:T(8,128)(2,1)}, u32[]{:S(2)}) copy-start(bf16[256,768]{1,0:T(8,128)(2,1)} %param.19) | copy-start | bytes 1179652
  138.1 13.4 %all-to-all-start = ((bf16[4,2,192,128]{3,1,2,0:T(2,128)(2,1)}), bf16[4,2,192,128]{3,1,2,0:T(2,128)(2,1)S(1)}, u32[]{:S(2)}, u32[]{:S(2)}) async-start(bf16[4,2,192,128]{3,1,2,0:T(2,128)(2,1)} %copy.64), calls=%async_computation | async-start | bytes 786432 | tf_op jit(solution)/shard_map/all_to_all | solution.py:356
  142.6 239.5 %reduce-scatter.9.cloned.1.call-start = ((), (), s32[]{:S(2)}) async-start(), calls=%async_computation.13 | async-start | bytes 7077888 | tf_op jit(solution)/shard_map/reduce_scatter | solution.py:387
  151.5 36.7 %copy-start.20 = (bf16[4,2,192,128]{3,1,2,0:T(2,128)(2,1)}, bf16[4,2,192,128]{3,1,2,0:T(2,128)(2,1)S(1)}, u32[]{:S(2)}) copy-start(bf16[4,2,192,128]{3,1,2,0:T(2,128)(2,1)S(1)} %all-to-all-done) | copy-start | bytes 1179652
  188.2 64.1 %copy-start.10 = (bf16[256,768]{1,0:T(8,128)(2,1)S(1)}, bf16[256,768]{1,0:T(8,128)(2,1)}, u32[]{:S(2)}) copy-start(bf16[256,768]{1,0:T(8,128)(2,1)} %param.20) | copy-start | bytes 1179652
  252.3 6.7 copy-start.5
  252.3 6.7 copy-start.27
  321.1 89.9 %reduce-scatter.19.cloned.1.call-start = ((), (), s32[]{:S(2)}) async-start(), calls=%async_computation.20 | async-start | bytes 1474560
  391.3 44.4 %reduce-scatter.13.cloned.1.call-start = ((), (), s32[]{:S(2)}) async-start(), calls=%async_computation.17 | async-start | bytes 1769472 | tf_op jit(solution)/shard_map/reduce_scatter | solution.py:399
  392.8 105.8 %reduce-scatter.15.cloned.1.call-start = ((), (), s32[]{:S(2)}) async-start(), calls=%async_computation.18 | async-start | bytes 7077888 | tf_op jit(solution)/shard_map/reduce_scatter | solution.py:399
  398.1 163.3 %reduce-scatter.17.cloned.1.call-start = ((), (), s32[]{:S(2)}) async-start(), calls=%async_computation.19 | async-start | bytes 7077888 | tf_op jit(solution)/shard_map/reduce_scatter | solution.py:399
  403.4 193.8 %all-reduce.5.cloned.1.call-start = ((), (), s32[]{:S(2)}) async-start(), calls=%async_computation.15 | async-start | bytes 884736 | tf_op jit(solution)/shard_map/psum | solution.py:400
  413.0 314.1 %all-reduce.7.cloned.1.call-start = ((), (), s32[]{:S(2)}) async-start(), calls=%async_computation.21 | async-start | bytes 10616832 | tf_op jit(solution)/shard_map/psum | solution.py:400
  561.4 203.5 %reduce-scatter.11.cloned.1.call-start = ((), (), s32[]{:S(2)}) async-start(), calls=%async_computation.14 | async-start | bytes 1966080 | tf_op jit(solution)/shard_map/reduce_scatter | solution.py:390
  566.4 251.6 %all-gather.18.cloned.1.call-start = ((), (), s32[]{:S(2)}) async-start(), calls=%async_computation.16 | async-start | bytes 2211840 | tf_op jit(solution)/shard_map/all_gather | solution.py:404
  733.8 34.0 %copy-start.8 = (f32[256,768]{1,0:T(8,128)S(1)}, f32[256,768]{1,0:T(8,128)}, u32[]{:S(2)}) copy-start(f32[256,768]{1,0:T(8,128)} %copy-done.7) | copy-start | bytes 2359300
  (20 other events, 44.9 us)
Sparse Core Ops, SparseCore 0:
  9.6 39.7 all-gather.7
  55.2 44.3 all-gather.9
  101.2 22.7 all-gather.11
  125.4 62.7 all-gather.13
  189.6 62.6 all-gather.15
  321.3 60.8 reduce-scatter.8
  391.4 19.5 reduce-scatter.18
  413.8 21.7 reduce-scatter.12
  438.6 59.9 reduce-scatter.14
  501.3 59.9 reduce-scatter.16
  564.5 32.7 all-reduce.4
  601.1 125.9 all-reduce.6
  729.5 35.3 reduce-scatter.10
  766.4 40.3 all-gather.17

commit v2 on v1

--- a/solution.py
+++ b/solution.py
@@ -22,13 +22,10 @@
 SCALE = 0.125
 MASKED = -1e30
 ROOT_HALF = 0.7071067811865476
+PDF_SCALE = 0.3989422804014327
 VMEM_LIMIT = 56 << 20
 bf16 = jnp.bfloat16
 f32 = jnp.float32
-
-
-def smooth_unit(values):
-    return 0.5 * values * (1.0 + jax.scipy.special.erf(values * ROOT_HALF))
 
 
 def layer_norm(values, gain, shift):
@@ -282,6 +279,414 @@
     )(where, text, low, high, q, kv, first, lse, grad_t, wide)
 
 
+MESH = pl.DeviceIdType.MESH
+
+
+def send(src, dst, out_sem, in_sem, **device):
+    return pltpu.make_async_remote_copy(
+        src_ref=src, dst_ref=dst, send_sem=out_sem, recv_sem=in_sem, device_id=device, device_id_type=MESH
+    )
+
+
+def place():
+    return tuple(lax.axis_index(name) for name in ("g", "r", "core", "x"))
+
+
+def seat(r, core, x):
+    return (r * 2 + core) * 2 + x
+
+
+def greet(g, r, core, x, line):
+    barrier = pltpu.get_barrier_semaphore()
+
+    def hello(**device):
+        pl.semaphore_signal(barrier, inc=1, device_id=device, device_id_type=MESH)
+
+    hello(core=1 - core)
+    hello(x=1 - x)
+    hello(r=1 - r)
+    if line:
+        for away in range(1, GROUPS):
+            hello(g=lax.rem(g + away, GROUPS))
+        pl.semaphore_wait(barrier, 3 + GROUPS - 1)
+    else:
+        pl.when(g > 0)(lambda: hello(g=g - 1))
+        pl.when(g < GROUPS - 1)(lambda: hello(g=g + 1))
+        pl.semaphore_wait(barrier, 5 - jnp.where(g == 0, 1, 0) - jnp.where(g == GROUPS - 1, 1, 0))
+
+
+NEAREST = tuple(tuple(sorted(range(GROUPS), key=lambda s: (abs(s - z), s))) for z in range(GROUPS))
+
+
+def nearest(g, step):
+    picked = NEAREST[0][step]
+    for z in range(1, GROUPS):
+        picked = jnp.where(g == z, NEAREST[z][step], picked)
+    return picked
+
+
+def gather_kernel(
+    tokens_ref, narrow_ref, small_ref, up_ref, down_ref, wo_ref,
+    kv_ref, q_ref, normed_ref, small_out, up_out, down_out, wo_out,
+    lined, wfull, small_in, kvs,
+    z_own, z_send, z_recv, s_sem, n_send, n_recv, kv_send, kv_recv, kv_local, w_send, w_recv, w_local,
+):
+    g, r, core, x = place()
+    other = 1 - x
+    rows, width = tokens_ref.shape
+    half = width // 2
+    fourth = half // 2
+    eighth = half // 4
+    greet(g, r, core, x, False)
+
+    def along(source, away, sem):
+        return send(lined.at[source], lined.at[source], sem, z_recv.at[source], g=g + away)
+
+    lined[g] = tokens_ref[...]
+    pl.when(g > 0)(lambda: along(g, -1, z_own.at[0]).start())
+    pl.when(g < GROUPS - 1)(lambda: along(g, 1, z_own.at[1]).start())
+
+    small_move = send(small_ref, small_in, s_sem.at[0], s_sem.at[1], x=other)
+    small_move.start()
+    mine = pl.ds(x * half + core * fourth, fourth)
+    narrow_x = send(narrow_ref.at[pl.ds(core * fourth, fourth)], wfull.at[mine], n_send.at[0], n_recv.at[0], x=other)
+    narrow_x.start()
+
+    def wo_rows(owner, part):
+        return wo_out.at[pl.ds(owner * half + core * fourth + part * eighth, eighth)]
+
+    def up_rows(owner, part):
+        return up_out.at[part, pl.ds(owner * half, half)]
+
+    def down_rows(owner, part):
+        return down_out.at[owner, pl.ds(part * half, half)]
+
+    wo_x = send(wo_ref.at[pl.ds(core * fourth + r * eighth, eighth)], wo_rows(x, r), w_send.at[0], w_recv.at[0], x=other)
+    up_x = send(
+        up_ref.at[:, pl.ds(pl.multiple_of((2 * r + core) * width, width), width)],
+        up_rows(x, r), w_send.at[1], w_recv.at[1], x=other,
+    )
+    down_x = send(down_ref.at[pl.ds(core * width + r * half, half)], down_rows(x, r), w_send.at[2], w_recv.at[2], x=other)
+    wo_y = send(wo_rows(other, r), wo_rows(other, r), w_send.at[3], w_recv.at[3], r=1 - r)
+    up_y = send(up_rows(other, r), up_rows(other, r), w_send.at[4], w_recv.at[4], r=1 - r)
+    down_y = send(down_rows(other, r), down_rows(other, r), w_send.at[5], w_recv.at[5], r=1 - r)
+    wo_s = [
+        send(wo_rows(other, part), wo_rows(other, part), w_send.at[6 + i], w_recv.at[6 + i], core=1 - core)
+        for i, part in enumerate((r, 1 - r))
+    ]
+    wo_x.start()
+    locals_ = [
+        pltpu.make_async_copy(wo_ref, wo_out.at[pl.ds(x * half, half)], w_local.at[0]),
+        pltpu.make_async_copy(down_ref.at[pl.ds(core * width, width)], down_out.at[x], w_local.at[1]),
+    ] + [
+        pltpu.make_async_copy(
+            up_ref.at[:, pl.ds(pl.multiple_of((2 * h + core) * width, width), width)],
+            up_out.at[h, pl.ds(x * half, half)], w_local.at[2 + h],
+        )
+        for h in range(2)
+    ]
+    for item in locals_:
+        item.start()
+
+    wfull[pl.ds(x * half, half)] = narrow_ref[...]
+    narrow_x.wait_recv()
+    theirs = wfull.at[pl.ds(other * half + core * fourth, fourth)]
+    narrow_s = send(theirs, theirs, n_send.at[1], n_recv.at[1], core=1 - core)
+    narrow_s.start()
+    small_move.wait_recv()
+    small_out[...] = small_ref[...] + small_in[...]
+    narrow_s.wait_recv()
+
+    own = seat(r, core, x)
+
+    def block(owner, source):
+        return kv_ref.at[owner, source]
+
+    def push(step, kind, what, **device):
+        copy = send(what[0], what[1], kv_send.at[kind, step], kv_recv.at[kind, step], **device)
+        copy.start()
+
+    def settle(step, kind, owner, source):
+        send(block(owner, source), block(owner, source), kv_send.at[kind, step], kv_recv.at[kind, step], x=other).wait_recv()
+
+    def forward(step):
+        source = nearest(g, step)
+        by_x = block(seat(r, core, other), source)
+        settle(step, 0, seat(r, core, other), source)
+        if step % 2 == 0:
+            push(step, 3, (by_x, by_x), r=1 - r)
+        push(step, 4, (by_x, by_x), core=1 - core)
+        by_y = block(seat(1 - r, core, x), source)
+        settle(step, 1, seat(1 - r, core, x), source)
+        if step % 2 == 1:
+            push(step, 3, (by_y, by_y), x=other)
+        push(step, 5, (by_y, by_y), core=1 - core)
+
+    def forward_far(step):
+        source = nearest(g, step)
+        far = block(seat(1 - r, core, other), source)
+        settle(step, 3, seat(1 - r, core, other), source)
+        push(step, 6, (far, far), core=1 - core)
+
+    for step in range(GROUPS):
+        source = nearest(g, step)
+        if step > 0:
+            send(lined.at[source], lined.at[source], z_send.at[source], z_recv.at[source], x=other).wait_recv()
+            pl.when((source < g) & (g < GROUPS - 1))(lambda: along(source, 1, z_send.at[source]).start())
+            pl.when((source > g) & (g > 0))(lambda: along(source, -1, z_send.at[source]).start())
+        values = lined[source].astype(f32)
+        normed = layer_norm(values, small_out[0:1], small_out[1:2]).astype(bf16)
+        normed_ref[source] = normed
+        both = dot(normed, wfull[...]) + small_out[12:13, : wfull.shape[1]]
+        q_ref[source] = (both[:, : 2 * BLK] * SCALE).astype(bf16)
+        kvs[step] = both[:, 2 * BLK :].astype(bf16)
+        here = (kvs.at[step], block(own, source))
+        push(step, 0, here, x=other)
+        push(step, 1, here, r=1 - r)
+        push(step, 2, here, core=1 - core)
+        pltpu.make_async_copy(kvs.at[step], block(own, source), kv_local.at[step]).start()
+        if step == 0:
+            up_x.start()
+        if step == GROUPS - 1:
+            down_x.start()
+        if step > 0:
+            forward(step - 1)
+        if step > 1:
+            forward_far(step - 2)
+    wo_x.wait_recv()
+    wo_y.start()
+    wo_s[0].start()
+    forward(GROUPS - 1)
+    forward_far(GROUPS - 2)
+    up_x.wait_recv()
+    up_y.start()
+    send(wo_rows(other, 1 - r), wo_rows(other, 1 - r), w_send.at[3], w_recv.at[3], r=1 - r).wait_recv()
+    wo_s[1].start()
+    forward_far(GROUPS - 1)
+    down_x.wait_recv()
+    down_y.start()
+
+    for step in range(GROUPS):
+        source = nearest(g, step)
+        pltpu.make_async_copy(kvs.at[step], block(own, source), kv_local.at[step]).wait()
+        settle(step, 2, seat(r, 1 - core, x), source)
+        settle(step, 4, seat(r, 1 - core, other), source)
+        settle(step, 5, seat(1 - r, 1 - core, x), source)
+        settle(step, 6, seat(1 - r, 1 - core, other), source)
+        for kind in range(7):
+            send(kvs.at[step], block(own, source), kv_send.at[kind, step], kv_recv.at[kind, step], x=other).wait_send()
+    pl.when(g > 0)(lambda: along(g, -1, z_own.at[0]).wait_send())
+    pl.when(g < GROUPS - 1)(lambda: along(g, 1, z_own.at[1]).wait_send())
+    for step in range(1, GROUPS):
+        source = nearest(g, step)
+        passed = ((source < g) & (g < GROUPS - 1)) | ((source > g) & (g > 0))
+        pl.when(passed)(lambda: send(lined.at[source], lined.at[source], z_send.at[source], z_recv.at[source], x=other).wait_send())
+    small_move.wait_send()
+    narrow_x.wait_send()
+    narrow_s.wait_send()
+    for item in locals_:
+        item.wait()
+    for item in (wo_x, up_x, down_x, wo_y, up_y, down_y, *wo_s):
+        item.wait_send()
+    send(up_rows(other, 1 - r), up_rows(other, 1 - r), w_send.at[4], w_recv.at[4], r=1 - r).wait_recv()
+    send(down_rows(other, 1 - r), down_rows(other, 1 - r), w_send.at[5], w_recv.at[5], r=1 - r).wait_recv()
+    for i, part in enumerate((r, 1 - r)):
+        there = wo_out.at[pl.ds(other * half + (1 - core) * fourth + part * eighth, eighth)]
+        send(there, there, w_send.at[6 + i], w_recv.at[6 + i], core=1 - core).wait_recv()
+
+
+def anywhere():
+    return pl.BlockSpec(memory_space=pl.ANY)
+
+
+def gather(tokens, narrow, small, up, down, wo):
+    rows, width = tokens.shape
+    wide = narrow.shape[1]
+    dma = pltpu.SemaphoreType.DMA
+    return pl.pallas_call(
+        gather_kernel,
+        out_shape=(
+            jax.ShapeDtypeStruct((8, GROUPS, rows, 2 * HW), bf16),
+            jax.ShapeDtypeStruct((GROUPS, rows, 2 * BLK), bf16),
+            jax.ShapeDtypeStruct((GROUPS, rows, width), bf16),
+            jax.ShapeDtypeStruct(small.shape, f32),
+            jax.ShapeDtypeStruct((2, width, width), bf16),
+            jax.ShapeDtypeStruct((2, width, width), bf16),
+            jax.ShapeDtypeStruct((width, width), bf16),
+        ),
+        in_specs=[whole_vmem()] * 3 + [anywhere()] * 3,
+        out_specs=(anywhere(), whole_vmem(), whole_vmem(), whole_vmem(), anywhere(), anywhere(), anywhere()),
+        scratch_shapes=[
+            pltpu.VMEM((GROUPS, rows, width), bf16),
+            pltpu.VMEM((width, wide), bf16),
+            pltpu.VMEM(small.shape, f32),
+            pltpu.VMEM((GROUPS, rows, 2 * HW), bf16),
+            dma((2,)), dma((GROUPS,)), dma((GROUPS,)), dma((2,)), dma((2,)), dma((2,)),
+            dma((7, GROUPS)), dma((7, GROUPS)), dma((GROUPS,)), dma((8,)), dma((8,)), dma((4,)),
+        ],
+        compiler_params=pltpu.CompilerParams(
+            collective_id=0, has_side_effects=True, vmem_limit_bytes=32 << 20
+        ),
+        name="gather",
+    )(tokens, narrow, small, up, down, wo)
+
+
+def erf_parts(values):
+    below = 0.5 * (1.0 + lax.erf(values * ROOT_HALF))
+    return below, PDF_SCALE * jnp.exp(-0.5 * values * values)
+
+
+def dense_kernel(
+    out_t_ref, tokens_ref, cot_ref, small_ref, up_ref, down_ref, wo_ref,
+    result_ref, middle_grad_ref, grad_t_ref, up_grad_ref, down_grad_ref, wo_grad_ref, sums_ref,
+    attn_in, attn_t, cots, h2s, mid_ref, n2_ref, part_y, part_d, in_y, in_d, hids, dus, grad_out,
+    a_send, a_recv, c_sem, h_sem, y_sem, d_sem, o_send, o_recv,
+):
+    g, r, core, x = place()
+    rows, width = tokens_ref.shape
+    greet(g, r, core, x, True)
+    cots[0] = cot_ref[...]
+    cot_move = send(cots.at[0], cots.at[1], c_sem.at[0], c_sem.at[1], core=1 - core)
+    cot_move.start()
+
+    def other_group(away):
+        return lax.rem(g + away, GROUPS)
+
+    attn_moves = []
+    for away in range(1, GROUPS):
+        to = other_group(away)
+        attn_moves.append(
+            send(out_t_ref.at[pl.ds(2 * to, 2)], attn_in.at[g], a_send.at[away], a_recv.at[g], g=to)
+        )
+        attn_moves[-1].start()
+    attn_in[g] = out_t_ref[pl.ds(2 * g, 2)]
+    sums_ref[...] = jnp.zeros_like(sums_ref)
+    sums_ref[5:6] = jnp.sum(cot_ref[...].astype(f32), axis=0, keepdims=True)
+    for away in range(1, GROUPS):
+        source = other_group(away)
+        send(attn_in.at[source], attn_in.at[source], a_send.at[away], a_recv.at[source], g=source).wait_recv()
+    for source in range(GROUPS):
+        attn_t[HW * source : HW * source + HW] = jnp.concatenate(
+            [attn_in[source, 0], attn_in[source, 1]], axis=1
+        )
+    middle = tokens_ref[...].astype(f32) + outer(attn_t[...], wo_ref[...]) + small_ref[2:3]
+    mid_ref[...] = middle
+    mean = jnp.mean(middle, axis=-1, keepdims=True)
+    centred = middle - mean
+    spread = jnp.mean(centred * centred, axis=-1, keepdims=True)
+    scale = lax.rsqrt(spread + EPS)
+    n2_ref[...] = centred * scale
+    h2s[0] = (n2_ref[...] * small_ref[3:4] + small_ref[4:5]).astype(bf16)
+    h2_move = send(h2s.at[0], h2s.at[1], h_sem.at[0], h_sem.at[1], core=1 - core)
+    h2_move.start()
+
+    for part in range(2):
+        if part == 1:
+            cot_move.wait_recv()
+            h2_move.wait_recv()
+        for h in range(2):
+            expanded = dot(h2s[part], up_ref[h]) + small_ref[pl.ds(8 + 2 * h + core, 1)]
+            below, density = erf_parts(expanded)
+            hidden = (expanded * below).astype(bf16)
+            hids[part, h] = hidden
+            slope = below + expanded * density
+            grad_hidden = inner(cots[part], down_ref[h]).astype(bf16).astype(f32)
+            grad_expand = (grad_hidden * slope).astype(bf16)
+            dus[part, h] = grad_expand
+            if h == 0:
+                part_y[part] = dot(hidden, down_ref[h])
+                part_d[part] = inner(grad_expand, up_ref[h])
+            else:
+                part_y[part] += dot(hidden, down_ref[h])
+                part_d[part] += inner(grad_expand, up_ref[h])
+            sums_ref[pl.ds(8 + 2 * h + core, 1)] += jnp.sum(
+                grad_expand.astype(f32), axis=0, keepdims=True
+            )
+    d_move = send(part_d.at[1], in_d, d_sem.at[0], d_sem.at[1], core=1 - core)
+    d_move.start()
+    y_move = send(part_y.at[1], in_y, y_sem.at[0], y_sem.at[1], core=1 - core)
+    y_move.start()
+    d_move.wait_recv()
+    grad_second = part_d[0] + in_d[...]
+    n2 = n2_ref[...]
+    sums_ref[3:4] = jnp.sum(grad_second * n2, axis=0, keepdims=True)
+    sums_ref[4:5] = jnp.sum(grad_second, axis=0, keepdims=True)
+    pulled = grad_second * small_ref[3:4]
+    inward = pulled - jnp.mean(pulled, axis=-1, keepdims=True) - n2 * jnp.mean(pulled * n2, axis=-1, keepdims=True)
+    grad_middle = cot_ref[...].astype(f32) + inward * scale
+    middle_grad_ref[...] = grad_middle
+    branch = grad_middle.astype(bf16)
+    sums_ref[2:3] = jnp.sum(branch.astype(f32), axis=0, keepdims=True)
+    grad_out_t = inner(wo_ref[...], branch).astype(bf16)
+    for group in range(GROUPS):
+        for b in range(2):
+            grad_out[group, b] = grad_out_t[HW * group : HW * group + HW, BLK * b : BLK * b + BLK]
+    grad_moves = []
+    for away in range(1, GROUPS):
+        to = other_group(away)
+        grad_moves.append(
+            send(grad_out.at[to], grad_t_ref.at[pl.ds(2 * g, 2)], o_send.at[away], o_recv.at[g], g=to)
+        )
+        grad_moves[-1].start()
+    grad_t_ref[pl.ds(2 * g, 2)] = grad_out[g]
+    y_move.wait_recv()
+    result_ref[...] = (mid_ref[...] + part_y[0] + in_y[...] + small_ref[5:6]).astype(bf16)
+    wo_grad_ref[...] = dot(attn_t[...], branch).astype(bf16)
+    for h in range(2):
+        down_grad_ref[h] = (outer(hids[0, h], cots[0]) + outer(hids[1, h], cots[1])).astype(bf16)
+        up_grad_ref[:, h * width : h * width + width] = (
+            outer(h2s[0], dus[0, h]) + outer(h2s[1], dus[1, h])
+        ).astype(bf16)
+    for away in range(1, GROUPS):
+        source = other_group(away)
+        send(
+            grad_t_ref.at[pl.ds(2 * source, 2)], grad_t_ref.at[pl.ds(2 * source, 2)],
+            o_send.at[away], o_recv.at[source], g=source,
+        ).wait_recv()
+    for item in (cot_move, h2_move, y_move, d_move, *attn_moves, *grad_moves):
+        item.wait_send()
+
+
+def dense(out_t, tokens, cot, small, up, down, wo):
+    rows, width = tokens.shape
+    dma = pltpu.SemaphoreType.DMA
+    full = (rows, width)
+    return pl.pallas_call(
+        dense_kernel,
+        out_shape=(
+            jax.ShapeDtypeStruct(full, bf16),
+            jax.ShapeDtypeStruct(full, f32),
+            jax.ShapeDtypeStruct(out_t.shape, bf16),
+            jax.ShapeDtypeStruct((width, 2 * width), bf16),
+            jax.ShapeDtypeStruct((2, width, width), bf16),
+            jax.ShapeDtypeStruct((width, width), bf16),
+            jax.ShapeDtypeStruct(small.shape, f32),
+        ),
+        in_specs=[whole_vmem()] * 7,
+        out_specs=(whole_vmem(),) * 7,
+        scratch_shapes=[
+            pltpu.VMEM((GROUPS, 2, HW, BLK), bf16),
+            pltpu.VMEM((width, rows), bf16),
+            pltpu.VMEM((2, *full), bf16),
+            pltpu.VMEM((2, *full), bf16),
+            pltpu.VMEM(full, f32),
+            pltpu.VMEM(full, f32),
+            pltpu.VMEM((2, *full), f32),
+            pltpu.VMEM((2, *full), f32),
+            pltpu.VMEM(full, f32),
+            pltpu.VMEM(full, f32),
+            pltpu.VMEM((2, 2, *full), bf16),
+            pltpu.VMEM((2, 2, *full), bf16),
+            pltpu.VMEM((GROUPS, 2, HW, BLK), bf16),
+            dma((GROUPS,)), dma((GROUPS,)), dma((2,)), dma((2,)), dma((2,)), dma((2,)), dma((GROUPS,)), dma((GROUPS,)),
+        ],
+        compiler_params=pltpu.CompilerParams(
+            collective_id=1, has_side_effects=True, vmem_limit_bytes=VMEM_LIMIT
+        ),
+        name="dense",
+    )(out_t, tokens, cot, small, up, down, wo)
+
+
 def pack_kv(key_part, value_part):
     return jnp.concatenate(
         [key_part, value_part[..., 2 * DH :], value_part[..., : 2 * DH]], axis=-1
@@ -292,8 +697,8 @@
     return both[..., :HW], jnp.concatenate([both[..., HW + DH :], both[..., HW : HW + DH]], axis=-1)
 
 
-ROWS = ("r", "core", "x")
-ALL = ("g", "r", "core", "x")
+ROWS = ("s", "r", "core", "x")
+ALL = ("g", "s", "r", "core", "x")
 
 
 def shards(
@@ -301,12 +706,11 @@
     key_weight, value_weight, value_bias, output_weight, output_bias, second_gain, second_shift,
     up_weight, up_bias, down_weight, down_bias,
 ):
-    def whole(item):
-        return lax.all_gather(item, "x", axis=0, tiled=True)
-
     rows, width = tokens.shape
+    half = width // 2
     group = lax.axis_index("g")
     rest = lax.axis_index(ROWS)
+    x = lax.axis_index("x")
     blocks = deal.shape[0]
     per_group = blocks // (2 * GROUPS)
 
@@ -318,71 +722,71 @@
     first = first_visible(positions, doc_lengths)
     low = first[:, 0] // CHUNK
     high = text // 2
+    first = first.reshape(2 * GROUPS, 1, BLK)
 
     def columns(item):
         return lax.dynamic_slice_in_dim(item, group * HW, HW, 1)
 
-    narrow = jnp.concatenate(
-        [columns(query_weight), columns(key_weight), columns(value_weight)], axis=1
-    )
-    narrow = whole(narrow)
-    wq, wk, wv = narrow[:, :HW], narrow[:, HW : 2 * HW], narrow[:, 2 * HW :]
-    small = whole(
-        jnp.stack([first_gain, first_shift, query_bias, value_bias, output_bias, second_gain, second_shift, down_bias], axis=1)
+    wq, wk, wv = columns(query_weight), columns(key_weight), columns(value_weight)
+    gap = jnp.zeros((half, 2 * BLK - HW), bf16)
+    narrow = jnp.concatenate([wq, gap, pack_kv(wk, wv)], axis=1)
+
+    def bias_part(item):
+        part = lax.dynamic_slice_in_dim(item, lax.rem(group, 2) * HW, HW)
+        return jnp.where(group // 2 == x, part, jnp.zeros_like(part))
+
+    query_part, value_part = bias_part(query_bias), bias_part(value_bias)
+    bias_row = jnp.concatenate(
+        [query_part, jnp.zeros((2 * BLK,), bf16), value_part[2 * DH :], value_part[: 2 * DH], jnp.zeros((BLK,), bf16)]
+    )
+    own_rows = jnp.stack(
+        [first_gain, first_shift, output_bias, second_gain, second_shift, down_bias, down_bias, down_bias]
+    )
+    place_rows = lax.dynamic_update_slice(jnp.zeros((8, width), bf16), own_rows, (0, x * half))
+    place_up = lax.dynamic_update_slice(
+        jnp.zeros((4, width), bf16), up_bias.reshape(2, width), (2 * x, 0)
+    )
+    small = jnp.concatenate(
+        [place_rows, place_up, bias_row[None], jnp.zeros((3, width), bf16)], axis=0
     ).astype(f32)
-    lower_gain, lower_shift, query_add, value_add, output_add, upper_gain, upper_shift, reduce_add = (
-        small[:, i] for i in range(8)
-    )
-    query_part = lax.dynamic_slice_in_dim(query_add, group * HW, HW)
-    value_part = lax.dynamic_slice_in_dim(value_add, group * HW, HW)
-    expand_add = whole(up_bias).astype(f32)
-    output_mat = whole(output_weight)
-    expand_mat = whole(up_weight)
-    reduce_mat = whole(down_weight)
-
-    lined = lax.all_gather(tokens, "g", axis=0, tiled=True).astype(f32)
-    normed = layer_norm(lined, lower_gain, lower_shift).astype(bf16)
-    q = ((dot(normed, wq) + query_part) * SCALE).astype(bf16)
-    k = dot(normed, wk).astype(bf16)
-    v = (dot(normed, wv) + value_part).astype(bf16)
-    kv = lax.all_gather(pack_kv(k, v), ROWS, axis=0, tiled=True)
+
+    kv, q, normed, small, up, down, wo = gather(
+        tokens, narrow, small, up_weight, down_weight, output_weight
+    )
+    kv = lax.all_gather(kv, "s", axis=0, tiled=True) if kv.shape[0] * 2 * GROUPS < blocks else kv
     kv = kv.reshape(blocks, BLK, 2 * HW)
-    q_pad = jnp.pad(q, ((0, 0), (0, 2 * BLK - HW))).reshape(2 * GROUPS, BLK, 2 * BLK)
-    first = first.reshape(2 * GROUPS, 1, BLK)
-    out_t, wide, lse = attend_forward(where, text, low, high, q_pad, kv, first)
-
-    def swap(item):
-        item = item.reshape(GROUPS, 2, HW, BLK)
-        return lax.all_to_all(item, "g", 0, 0, tiled=True)
-
-    attn_t = swap(out_t).transpose(0, 2, 1, 3).reshape(width, rows)
-
+    q = q.reshape(2 * GROUPS, BLK, 2 * BLK)
+    out_t, wide, lse = attend_forward(where, text, low, high, q, kv, first)
+    result, grad_middle, grad_t, up_grad, down_grad, wo_grad, sums = dense(
+        out_t, tokens, cotangent, small, up, down, wo
+    )
+
+    across = ("x", "g", "s", "r")
+    count = 2 * blocks // 8
+    up_own = lax.psum_scatter(
+        up_grad.reshape(count, -1, 2 * width), across, scatter_dimension=0, tiled=True
+    )
+    down_own = lax.psum_scatter(
+        down_grad.reshape(count, -1, width), across, scatter_dimension=0, tiled=True
+    )
+    wo_own = lax.psum_scatter(
+        wo_grad.reshape(2 * count, -1, width), (*across, "core"), scatter_dimension=0, tiled=True
+    )
+    up_own = lax.all_gather(up_own, ("g", "s", "r", "core"), axis=0, tiled=True)
+    up_own = (
+        up_own.reshape(count // 2, 2, -1, 2, width).transpose(0, 2, 3, 1, 4).reshape(half, 4 * width)
+    )
+    down_own = lax.all_gather(down_own, ("core", "g", "s", "r"), axis=0, tiled=True).reshape(-1, width)
+    wo_own = lax.all_gather(wo_own, ("g", "s", "r", "core"), axis=0, tiled=True).reshape(-1, width)
+
+    dq, dkv = attend_backward(where, text, low, high, q, kv, first, lse, grad_t, wide)
+    narrow_all = lax.all_gather(narrow, "x", axis=0, tiled=True)
+    wq = narrow_all[:, :HW]
+    wk, wv = unpack_kv(narrow_all[:, 2 * BLK :])
+    normed = normed.reshape(GROUPS * rows, width)
     inputs = tokens.astype(f32)
-    middle = inputs + outer(attn_t, output_mat) + output_add
-    second_normed = layer_norm(middle, upper_gain, upper_shift).astype(bf16)
-    expanded = dot(second_normed, expand_mat) + expand_add
-    hidden = smooth_unit(expanded).astype(bf16)
-    result = (middle + dot(hidden, reduce_mat) + reduce_add).astype(bf16)
-    grad_in = cotangent.astype(f32)
-    term_reduce_mat = outer(hidden, cotangent)
-    term_reduce_add = jnp.sum(grad_in, axis=0)
-    grad_hidden = inner(cotangent, reduce_mat).astype(bf16)
-    _, pull_unit = jax.vjp(smooth_unit, expanded)
-    grad_expand = pull_unit(grad_hidden.astype(f32))[0].astype(bf16)
-    term_expand_mat = outer(second_normed, grad_expand)
-    term_expand_add = jnp.sum(grad_expand.astype(f32), axis=0)
-    grad_second = inner(grad_expand, expand_mat)
-    _, pull_second = jax.vjp(layer_norm, middle, upper_gain, upper_shift)
-    grad_middle_part, term_upper_gain, term_upper_shift = pull_second(grad_second)
-    grad_middle = grad_in + grad_middle_part
-    grad_branch = grad_middle.astype(bf16)
-    term_output_mat = dot(attn_t, grad_branch)
-    term_output_add = jnp.sum(grad_branch.astype(f32), axis=0)
-    grad_mixed_t = inner(output_mat, grad_branch).astype(bf16)
-
-    grad_t = swap(grad_mixed_t.reshape(GROUPS, HW, 2, BLK).transpose(0, 2, 1, 3))
-    grad_t = grad_t.reshape(2 * GROUPS, HW, BLK)
-    dq, dkv = attend_backward(where, text, low, high, q_pad, kv, first, lse, grad_t, wide)
+    lower_gain, lower_shift = small[0], small[1]
+
     dq = dq.reshape(-1, 2 * BLK)[:, :HW] * bf16(SCALE)
     dkv = lax.psum_scatter(dkv.reshape(-1, 2 * HW), ROWS, scatter_dimension=0, tiled=True)
     dk, dv = unpack_kv(dkv)
@@ -395,58 +799,59 @@
     grad_input_part, term_lower_gain, term_lower_shift = pull_first(grad_first)
     grad_tokens = grad_middle + grad_input_part
 
-    def owned(item, axes):
-        mine = lax.psum_scatter(item.astype(bf16), "x", scatter_dimension=0, tiled=True)
-        return lax.psum(mine, axes).astype(f32)
-
-    ctx = ("g", "r", "core")
-    narrow_own = owned(term_narrow, ("r", "core"))
-    narrow_own = lax.all_gather(narrow_own.astype(bf16), "g").astype(f32)
+    narrow_own = lax.psum_scatter(term_narrow, "x", scatter_dimension=0, tiled=True)
+    narrow_own = lax.psum(narrow_own, ("s", "r", "core"))
+    narrow_own = lax.all_gather(narrow_own, "g").astype(f32)
     query_own, key_own, value_own = (
         narrow_own[:, :, i * HW : (i + 1) * HW].transpose(1, 0, 2).reshape(-1, width)
         for i in range(3)
     )
-    half = lax.axis_index("x") * (width // 2)
 
     def own_half(item):
-        return lax.dynamic_slice_in_dim(item, half, width // 2)
-
-    vectors = jnp.stack(
-        [
-            term_lower_gain, term_lower_shift, term_output_add, term_upper_gain, term_upper_shift, term_reduce_add,
-            lax.dynamic_update_slice_in_dim(jnp.zeros((width,), f32), term_query_add, group * HW, 0),
-            lax.dynamic_update_slice_in_dim(jnp.zeros((width,), f32), term_value_add, group * HW, 0),
-        ]
-        + [term_expand_add[i * width : (i + 1) * width] for i in range(4)]
-    )
-    vectors = lax.psum(vectors, ALL)
-    expand_own = lax.dynamic_slice_in_dim(
-        vectors[8:].reshape(-1), lax.axis_index("x") * (2 * width), 2 * width
-    )
+        return lax.dynamic_slice_in_dim(item, x * half, half)
+
+    spread = jnp.zeros((width,), f32)
+    sums = lax.psum(
+        jnp.concatenate(
+            [
+                sums,
+                jnp.stack(
+                    [
+                        term_lower_gain,
+                        term_lower_shift,
+                        lax.dynamic_update_slice_in_dim(spread, term_query_add, group * HW, 0),
+                        lax.dynamic_update_slice_in_dim(spread, term_value_add, group * HW, 0),
+                    ]
+                ),
+            ]
+        ),
+        ALL,
+    )
+    expand_own = lax.dynamic_slice_in_dim(sums, 8 + 2 * x, 2).reshape(-1)
     return (
         result,
         grad_tokens,
-        own_half(vectors[0]),
-        own_half(vectors[1]),
+        own_half(sums[16]),
+        own_half(sums[17]),
         query_own,
-        own_half(vectors[6]),
+        own_half(sums[18]),
         key_own,
         value_own,
-        own_half(vectors[7]),
-        owned(term_output_mat, ctx),
-        own_half(vectors[2]),
-        own_half(vectors[3]),
-        own_half(vectors[4]),
-        owned(term_expand_mat, ctx),
+        own_half(sums[19]),
+        wo_own.astype(f32),
+        own_half(sums[2]),
+        own_half(sums[3]),
+        own_half(sums[4]),
+        up_own.astype(f32),
         expand_own,
-        owned(term_reduce_mat, ctx),
-        own_half(vectors[5]),
+        down_own.astype(f32),
+        own_half(sums[5]),
     )
 
 
 def solution(mesh):
     devices = mesh.devices
-    inner_mesh = Mesh(devices.reshape(GROUPS, devices.shape[0] // (2 * GROUPS), 2, 2), ALL)
+    inner_mesh = Mesh(devices.reshape(GROUPS, devices.shape[0] // (4 * GROUPS), 2, 2, 2), ALL)
     row = P(ALL, None)
     mat = P("x", None)
     vec = P("x")

time: 834 us -> 914 us (1.096)
  Pallas kernels: 63.8 us -> 177 us
  matrix products: 43.5 us -> 6.44 us
  local copies, waits for them, and re-layouts: 50.2 us -> 72 us
    reduce_scatter x3, waiting for transfers between devices: 148 us -> 364 us  [the longest x1 132 us: shards(): lax.psum_scatter(down_grad.reshape(count, -1, width), across, scatter_dim...]
    psum x2 -> x1, waiting for transfers between devices: 155 us -> 17.5 us  [shards(): narrow_own = lax.psum(narrow_own, ('s', 'r', 'core'))]
    pallas_call x0 -> x2, Pallas kernels: none -> 130 us  [the longest x1 87.5 us: gather(): pl.pallas_call(gather_kernel, out_shape=(jax.ShapeDtypeStruct((8, GROUPS,...]
    all_gather x6 -> x3, waiting for transfers between devices: 145 us -> 43.7 us  [the longest x1 22.2 us: shards(): lax.all_gather(down_own, ('core', 'g', 's', 'r'), axis=0, tiled=True)]
    convert_element_type x1 -> x3, local copies, waits for them, and re-layouts: 1.91 us -> 21.4 us  [shards(): up_own.astype(f32)]
    all_to_all x1 -> x0, blocking collectives: 16.3 us -> none  [swap(): return lax.all_to_all(item, 'g', 0, 0, tiled=True)]
    dot_general x6 -> x0, matrix products: 15.3 us -> none  [dot(): return jnp.dot(left, right, preferred_element_type=f32)]
    dot_general x4 -> x1, matrix products: 15.6 us -> 3.32 us  [outer(): lax.dot_general(left, right, (((0,), (0,)), ((), ())), preferred_element_...]
  transfers between devices with their start and end apart: 15 -> 10, of which waited for: 13 -> 9; matrix products, arithmetic and copies ran while one was open for 9% -> 5% of each run, Pallas kernels for 3% -> 0%
where the time goes in v2:
time: 914 us; the launch traced here: 912 us
  waiting for transfers between devices  547 us (60%)
  Pallas kernels  177 us (19%)
  blocking collectives  76.9 us (8%)
  local copies, waits for them, and re-layouts  72 us (8%)
  other arithmetic  16.2 us (2%)
  between operations  14.5 us (2%)
    reduce_scatter x1, waiting for transfers between devices, shards(): lax.psum_scatter(down_grad.reshape(count, -1, width), across, scatter_dim...  132 us
    reduce_scatter x1, waiting for transfers between devices, shards(): lax.psum_scatter(up_grad.reshape(count, -1, 2 * width), across, scatter_d...  130 us
    reduce_scatter x1, waiting for transfers between devices, shards(): lax.psum_scatter(wo_grad.reshape(2 * count, -1, width), (*across, 'core')...  102 us
    pallas_call x1, Pallas kernels, gather(): pl.pallas_call(gather_kernel, out_shape=(jax.ShapeDtypeStruct((8, GROUPS,...  87.5 us
    reduce_scatter x1, waiting for transfers between devices, shards(): lax.psum_scatter(dkv.reshape(-1, 2 * HW), ROWS, scatter_dimension=0, tile...  69.8 us
    psum x1, blocking collectives, shards(): lax.psum(jnp.concatenate([sums, jnp.stack([term_lower_gain, term_lower_sh...  42.4 us
    pallas_call x1, Pallas kernels, dense(): pl.pallas_call(dense_kernel, out_shape=(jax.ShapeDtypeStruct(full, bf16),...  42.2 us
    reduce_scatter x1, waiting for transfers between devices, shards(): lax.psum_scatter(grad_first, 'g', scatter_dimension=0, tiled=True)  32 us
  transfers between devices with their start and end apart: 10, of which 9 were waited for; matrix products, arithmetic and copies ran while one was open for 5% of the time, Pallas kernels for 0%

profile of v2, /device:TPU:0, one launch (start us, length us, event | category | flops | bytes accessed | tf_op | source)
XLA Modules:
  0.0 911.5 jit_solution(9315357352397724537)
XLA Ops:
  29.3 87.5 %gather.1 = (bf16[8,4,256,384]{3,2,1,0:T(8,128)(2,1)S(1)}, bf16[4,256,256]{2,1,0:T(8,128)(2,1)S(1)}, bf16[4,256,768]{2,1,0:T(8,128)(2,1)S(1)}, f32[16,768]{1,0:T...) custom-call(bf16[256,768]{1,0:T(8,128)(2,1)S(1)} %copy-done.3, ...), custom_call_target="tpu_custom_call" | custom-call | tf_op jit(solution)/shard_map/gather/pallas_call | solution.py:506
  116.8 2.7 copy-done.2
  125.9 19.8 %attend_forward.1 = (bf16[8,192,128]{2,1,0:T(8,128)(2,1)}, f32[8,192,128]{2,1,0:T(8,128)}, f32[8,1,384]{2,1,0:T(1,128)}) custom-call(s32[64]{0:T(128)} %select_reduce_fusion.where_ref, s32[8]{0:T(128)} %copy-done.20, s32[8]{0:T(128)} %and_select_fusion.1.low_ref, s32[8]{0:T(128)} %get-tuple-element.128.high_ref, bf16[8,128,256]{2,1,0:T(8,128)(2,1)} %bitcast.34, ...), custom_call_target="tpu_custom_call" | custom-call | tf_op jit(solution)/shard_map/attend_forward/pallas_call | solution.py:150
  145.7 42.2 %dense.1 = (bf16[256,768]{1,0:T(8,128)(2,1)}, f32[256,768]{1,0:T(8,128)}, bf16[8,192,128]{2,1,0:T(8,128)(2,1)}, bf16[768,1536]{1,0:T(8,128)(2,1)}, bf16[2,768,76...) custom-call(bf16[8,192,128]{2,1,0:T(8,128)(2,1)} %get-tuple-element.38.out_t_ref, ...), custom_call_target="tpu_custom_call" | custom-call | tf_op jit(solution)/shard_map/dense/pallas_call | solution.py:654
  187.9 28.0 %attend_backward.1 = (bf16[8,128,256]{2,1,0:T(8,128)(2,1)}, bf16[64,128,384]{2,1,0:T(8,128)(2,1)}) custom-call(s32[64]{0:T(128)} %select_reduce_fusion.where_ref, s32[8]{0:T(128)} %copy-done.20, s32[8]{0:T(128)} %and_select_fusion.1.low_ref, s32[8]{0:T(128)} %get-tuple-element.128.high_ref, bf16[8,128,256]{2,1,0:T(8,128)(2,1)} %bitcast.35, ...), custom_call_target="tpu_custom_call" | custom-call | tf_op jit(solution)/shard_map/attend_backward/pallas_call | solution.py:259
  217.8 69.8 %reduce-scatter.9.cloned.1.call-done = bf16[1024,384]{1,0:T(8,128)(2,1)} async-done(((bf16[8192,384]{1,0:T(8,128)(2,1)}), bf16[1024,384]{1,0:T(8,128)(2,1)}) %reduce-scatter.9.cloned.1.call-update) | async-done | bytes 786448 | tf_op jit(solution)/shard_map/reduce_scatter | solution.py:791
  290.8 3.3 convolution_convert_fusion
  297.7 18.4 %reduce-scatter.19.cloned.1.call-done = bf16[384,576]{1,0:T(8,128)(2,1)} async-done(((bf16[768,576]{1,0:T(8,128)(2,1)}), bf16[384,576]{1,0:T(8,128)(2,1)}) %reduce-scatter.19.cloned.1.call-update) | async-done | bytes 442384
  318.7 129.9 %reduce-scatter.15.cloned.1.call-done = bf16[1,48,1536]{2,1,0:T(8,128)(2,1)} async-done(((bf16[16,48,1536]{2,1,0:T(8,128)(2,1)}), bf16[1,48,1536]{2,1,0:T(8,128)(2,1)}) %reduce-scatter.15.cloned.1.call-update) | async-done | bytes 147472 | tf_op jit(solution)/shard_map/reduce_scatter | solution.py:766
  448.7 132.1 %reduce-scatter.17.cloned.1.call-done = bf16[1,96,768]{2,1,0:T(8,128)(2,1)} async-done(((bf16[16,96,768]{2,1,0:T(8,128)(2,1)}), bf16[1,96,768]{2,1,0:T(8,128)(2,1)}) %reduce-scatter.17.cloned.1.call-update) | async-done | bytes 147472 | tf_op jit(solution)/shard_map/reduce_scatter | solution.py:769
  580.9 12.1 %all_gather.18 = bf16[768,640]{1,0:T(8,128)(2,1)S(1)} all-gather(bf16[384,640]{1,0:T(8,128)(2,1)S(1)} %concatenate.22.narrow_ref), channel_id=1, replica_groups=mesh['g'=4,'s'=1,'r'=2,'core'=2,'x'=2] {'x'}, dimensions={0}, use_global_device_ids=true | all-gather | bytes 1474560 | tf_op jit(solution)/shard_map/all_gather | solution.py:783
  598.0 17.5 %all-reduce.2.cloned.1.call-done = bf16[1,384,576]{1,2,0:T(8,128)(2,1)} async-done(((bf16[1,384,576]{1,2,0:T(8,128)(2,1)}), bf16[1,384,576]{1,2,0:T(8,128)(2,1)}) %all-reduce.2.cloned.1.call-update) | async-done | bytes 442384 | tf_op jit(solution)/shard_map/psum | solution.py:803
  615.5 102.1 %reduce-scatter.13.cloned.1.call-done = bf16[1,24,768]{2,1,0:T(8,128)(2,1)} async-done(((bf16[32,24,768]{2,1,0:T(8,128)(2,1)}), bf16[1,24,768]{2,1,0:T(8,128)(2,1)}) %reduce-scatter.13.cloned.1.call-update) | async-done | bytes 36880 | tf_op jit(solution)/shard_map/reduce_scatter | solution.py:772
  717.7 22.3 %all_gather.21 = bf16[16,24,768]{2,1,0:T(8,128)(2,1)S(1)} all-gather(bf16[1,24,768]{2,1,0:T(8,128)(2,1)} %reduce-scatter.13.cloned.1.call-done), channel_id=1, replica_groups=mesh['g'=4,'s'=1,'r'=2,'core'=2,'x'=2] {'g','s','r','core'}, dimensions={0}, use_global_device_ids=true | all-gather | bytes 626688 | tf_op jit(solution)/shard_map/all_gather | solution.py:780
  741.1 21.5 %all-gather.6.cloned.1.call-done = bf16[16,48,1536]{2,1,0:T(8,128)(2,1)} async-done(((bf16[1,48,1536]{2,1,0:T(8,128)(2,1)}), bf16[16,48,1536]{2,1,0:T(8,128)(2,1)}) %all-gather.6.cloned.1.call-update) | async-done | bytes 2359312 | tf_op jit(solution)/shard_map/all_gather | solution.py:775
  762.6 6.2 reshape.220
  768.9 8.1 copy.52
  777.0 7.0 reshape.218
  784.0 22.2 %all-gather.8.cloned.1.call-done = bf16[16,96,768]{2,1,0:T(8,128)(2,1)} async-done(((bf16[1,96,768]{2,1,0:T(8,128)(2,1)}), bf16[16,96,768]{2,1,0:T(8,128)(2,1)}) %all-gather.8.cloned.1.call-update) | async-done | bytes 2359312 | tf_op jit(solution)/shard_map/all_gather | solution.py:779
  806.2 4.2 bitcast_convert_fusion
  810.7 32.0 %reduce-scatter.11.cloned.1.call-done = bf16[256,768]{1,0:T(8,128)(2,1)} async-done(((bf16[1024,768]{1,0:T(8,128)(2,1)}), bf16[256,768]{1,0:T(8,128)(2,1)}) %reduce-scatter.11.cloned.1.call-update) | async-done | bytes 393232 | tf_op jit(solution)/shard_map/reduce_scatter | solution.py:794
  845.7 42.4 %psum.14 = f32[20,768]{1,0:T(8,128)S(1)} all-reduce(f32[20,768]{1,0:T(8,128)S(1)} %concatenate.27), channel_id=1, replica_groups=mesh['g'=4,'s'=1,'r'=2,'core'=2,'x'=2] {'g','s','r','core','x'}, use_global_device_ids=true, to_apply=%region_13.14 | all-reduce | flops 15360 | bytes 122880 | tf_op jit(solution)/shard_map/psum | solution.py:814
  895.8 2.8 fusion.35
  898.5 2.7 copy.53
  (144 shorter events, 60.1 us)
Async XLA Ops:
  7.2 8.2 copy-start
  7.2 19.3 %copy-start.3 = (bf16[256,768]{1,0:T(8,128)(2,1)S(1)}, bf16[256,768]{1,0:T(8,128)(2,1)}, u32[]{:S(2)}) copy-start(bf16[256,768]{1,0:T(8,128)(2,1)} %tokens_ref.3) | copy-start | bytes 1179652
  7.2 19.3 %copy-start.5 = (bf16[384,3072]{1,0:T(8,128)(2,1)S(1)}, bf16[384,3072]{1,0:T(8,128)(2,1)}, u32[]{:S(2)}) copy-start(bf16[384,3072]{1,0:T(8,128)(2,1)} %up_ref.1) | copy-start | bytes 7077892
  7.2 280.4 %reduce-scatter.9.cloned.1.call-start = ((), (), s32[]{:S(2)}) async-start(), calls=%async_computation.6 | async-start | bytes 7077888 | tf_op jit(solution)/shard_map/reduce_scatter | solution.py:791
  26.6 1.7 copy-start.6
  116.8 2.7 copy-start.2
  119.5 1.4 copy-start.7
  120.9 1.4 copy-start.8
  124.7 1.2 copy-start.13
  215.9 74.8 %copy-start.14 = (bf16[4,256,768]{2,1,0:T(8,128)(2,1)S(1)}, bf16[4,256,768]{2,1,0:T(8,128)(2,1)}, u32[]{:S(2)}) copy-start(bf16[4,256,768]{2,1,0:T(8,128)(2,1)} %copy-done.13) | copy-start | bytes 4718596
  215.9 100.2 %reduce-scatter.19.cloned.1.call-start = ((), (), s32[]{:S(2)}) async-start(), calls=%async_computation.15 | async-start | bytes 1474560
  296.3 152.3 %reduce-scatter.15.cloned.1.call-start = ((), (), s32[]{:S(2)}) async-start(), calls=%async_computation.11 | async-start | bytes 2506752 | tf_op jit(solution)/shard_map/reduce_scatter | solution.py:766
  297.1 283.7 %reduce-scatter.17.cloned.1.call-start = ((), (), s32[]{:S(2)}) async-start(), calls=%async_computation.13 | async-start | bytes 2506752 | tf_op jit(solution)/shard_map/reduce_scatter | solution.py:769
  297.7 317.8 %all-reduce.2.cloned.1.call-start = ((), (), s32[]{:S(2)}) async-start(), calls=%async_computation.8 | async-start | bytes 884736 | tf_op jit(solution)/shard_map/psum | solution.py:803
  318.1 399.6 %reduce-scatter.13.cloned.1.call-start = ((), (), s32[]{:S(2)}) async-start(), calls=%async_computation.10 | async-start | bytes 1216512 | tf_op jit(solution)/shard_map/reduce_scatter | solution.py:772
  318.7 444.0 %all-gather.6.cloned.1.call-start = ((), (), s32[]{:S(2)}) async-start(), calls=%async_computation.12 | async-start | bytes 2506752 | tf_op jit(solution)/shard_map/all_gather | solution.py:775
  448.6 357.5 %all-gather.8.cloned.1.call-start = ((), (), s32[]{:S(2)}) async-start(), calls=%async_computation.14 | async-start | bytes 2506752 | tf_op jit(solution)/shard_map/all_gather | solution.py:779
  580.8 261.8 %reduce-scatter.11.cloned.1.call-start = ((), (), s32[]{:S(2)}) async-start(), calls=%async_computation.7 | async-start | bytes 1966080 | tf_op jit(solution)/shard_map/reduce_scatter | solution.py:794
  596.6 1.2 copy-start.4
  596.6 299.1 %all-gather.4.cloned.1.call-start = ((), (), s32[]{:S(2)}) async-start(), calls=%async_computation.9 | async-start | bytes 2211840 | tf_op jit(solution)/shard_map/all_gather | solution.py:804
  784.0 61.6 %copy-start.19 = (f32[16,768]{1,0:T(8,128)S(1)}, f32[16,768]{1,0:T(8,128)}, u32[]{:S(2)}) copy-start(f32[16,768]{1,0:T(8,128)} %get-tuple-element.50) | copy-start | bytes 147460
  810.4 83.2 %copy-start.17 = (f32[256,768]{1,0:T(8,128)S(1)}, f32[256,768]{1,0:T(8,128)}, u32[]{:S(2)}) copy-start(f32[256,768]{1,0:T(8,128)} %get-tuple-element.44) | copy-start | bytes 2359300
  901.2 3.5 copy-start.1
  901.2 2.8 copy-start.18
  (7 other events, 6.2 us)
Sparse Core Ops, SparseCore 0:
  216.0 71.5 reduce-scatter.8
  296.5 19.5 reduce-scatter.18
  321.0 127.5 reduce-scatter.14
  454.1 126.6 reduce-scatter.16
  583.6 31.8 all-reduce.1
  621.2 96.3 reduce-scatter.12
  720.2 42.3 all-gather.5
  765.1 41.0 all-gather.7
  808.6 34.0 reduce-scatter.10
  844.2 40.3 all-gather.3
